TPU v7x, 256 devices: a whole 4x4x8 slice. The times are simulated.
256 devices in a mesh: pb: 16 (over z, core), kv: 16 (over y, x).
Axes of the slice: x: 4, y: 4, z: 8, core: 2. Of those that a mesh axis runs over, the one named last changes fastest.
Arguments:
- queries: bfloat16 [393216, 1024], P(('pb', 'kv')), may hold values from -8 to 8
- keys: bfloat16 [524288, 128], P(('kv', 'pb')), may hold values from -6 to 6
- values: bfloat16 [524288, 128], P(('kv', 'pb')), may hold values from -6 to 6
- selected: int32 [6144, 14], P(('pb', 'kv')), may hold values from 1 to 8190, as said below
Outputs:
- attended: bfloat16 [393216, 1024], P(('pb', 'kv'))
Inputs may be any that keep to these rules, and one draw needn't show every extreme that they name: `selected`: each row names 14 different blocks, never block 0 or block 8191. Key device k holds blocks k * 32 to (k + 1) * 32 - 1, devices counted with kv slowest; query device d holds query blocks d * 24 to (d + 1) * 24 - 1, devices counted with pb slowest. The query blocks of one device name together at most 2 distinct blocks of one key device, and in every draw some key device has exactly 2 named by every query device.
All inputs are finite; a program needn't handle non-finite values.
Results may differ from a plain program's by a relative error of at most 0.0046.
Values may be sent and summed in bfloat16 or wider, within the bound.
A program may use at most 128 MiB of HBM per device.

v0:
```python
import math

import jax
import jax.numpy as jnp
from jax import lax
from jax.sharding import PartitionSpec as P

H = 8
DH = 128
BLOCK = 64
TOPN = 16
QB = 64
CAP = 2


def broadcast(value, axis, root):
    mine = lax.axis_index(axis) == root
    return lax.psum(jnp.where(mine, value, jnp.zeros_like(value)), axis)


def holdings(wanted, owner, blocks_here):
    local_ids = owner * blocks_here + jnp.arange(blocks_here, dtype=jnp.int32)
    hits = (wanted[:, None] == local_ids[None, :]).astype(jnp.int32)
    present = jnp.max(hits, axis=0)
    return (present, jnp.cumsum(present) - present)


def slot_lists(present, slot_rank, slots):
    local_ids = jnp.arange(present.shape[-1], dtype=jnp.int32)
    slot_ids = jnp.arange(slots, dtype=jnp.int32)
    matches = (present[..., :, None] == 1) & (slot_rank[..., :, None] == slot_ids)
    return jnp.sum(jnp.where(matches, local_ids[:, None], 0), axis=-2)


def per_device(queries, keys, values, selected):
    pb_count = lax.axis_size("pb")
    kv_count = lax.axis_size("kv")
    devices = pb_count * kv_count
    blocks_here = keys.shape[0] // BLOCK
    query_blocks = queries.shape[0] // QB
    tiles_local = jnp.concatenate(
        [keys.reshape(blocks_here, BLOCK, DH), values.reshape(blocks_here, BLOCK, DH)], axis=2
    )
    slots = CAP
    wanted = selected.reshape(-1)
    owners = jnp.arange(devices, dtype=jnp.int32)
    present, slot_rank = jax.vmap(lambda owner: holdings(wanted, owner, blocks_here))(owners)
    owner_lists = slot_lists(present, slot_rank, slots)
    by_axes = owner_lists.reshape(kv_count, pb_count, slots).transpose(1, 0, 2)
    asked_for = lax.all_to_all(
        lax.all_to_all(by_axes, "pb", split_axis=0, concat_axis=0, tiled=True),
        "kv",
        split_axis=1,
        concat_axis=1,
        tiled=True,
    )
    outgoing = jnp.take(tiles_local, asked_for.reshape(-1), axis=0).reshape(
        pb_count, kv_count, slots, BLOCK, 2 * DH
    )
    fetched = lax.all_to_all(
        lax.all_to_all(outgoing, "pb", split_axis=0, concat_axis=0, tiled=True),
        "kv",
        split_axis=1,
        concat_axis=1,
        tiled=True,
    )
    tile_table = fetched.reshape(devices * slots, BLOCK, 2 * DH)
    owner_of = selected // blocks_here
    positions = (owner_of % pb_count * kv_count + owner_of // pb_count) * slots + jnp.take(
        slot_rank.reshape(-1), selected
    )
    first_tile = broadcast(tiles_local[:1], ("pb", "kv"), 0)
    latest = broadcast(tiles_local[blocks_here - 1 :], ("pb", "kv"), devices - 1)
    tile_table = jnp.concatenate([tile_table, first_tile, latest], axis=0)
    extra_base = devices * slots
    leading_positions = jnp.broadcast_to(
        jnp.array([extra_base, extra_base + 1], jnp.int32), (query_blocks, 2)
    )
    positions = jnp.concatenate([leading_positions, positions], axis=1)
    group_size = math.gcd(query_blocks, 8)
    q_groups = queries.reshape(query_blocks // group_size, group_size, QB * H, DH)
    p_groups = positions.reshape(query_blocks // group_size, group_size, TOPN)

    def attend(operands):
        q_block, positions_in = operands
        gathered = jnp.take(tile_table, positions_in.reshape(-1), axis=0).reshape(
            group_size, TOPN * BLOCK, 2 * DH
        )
        scores = jnp.einsum(
            "gqd,gkd->gqk", q_block, gathered[..., :DH], preferred_element_type=jnp.float32
        ) * DH ** (-0.5)
        weights = jnp.exp(scores - jnp.max(scores, axis=-1, keepdims=True))
        totals = jnp.sum(weights, axis=-1, keepdims=True)
        weighted = jnp.einsum(
            "gqk,gkd->gqd",
            weights.astype(jnp.bfloat16),
            gathered[..., DH:],
            preferred_element_type=jnp.float32,
        )
        return (weighted / totals).astype(jnp.bfloat16)

    result = lax.map(attend, (q_groups, p_groups))
    return result.reshape(query_blocks * QB, H * DH)


def solution(mesh):
    placed = (
        P(("pb", "kv"), None),
        P(("kv", "pb"), None),
        P(("kv", "pb"), None),
        P(("pb", "kv"), None),
    )
    return jax.shard_map(
        per_device, mesh=mesh, in_specs=placed, out_specs=P(("pb", "kv"), None), check_vma=False
    )
```

profile of v0, /device:TPU:12, one launch (start us, length us, event | category | flops | bytes accessed | tf_op | source)
XLA Modules:
  0.0 932.5 jit_solution(3623910404846668406)
XLA Ops:
  9.4 16.0 %all_to_all.20 = s32[16,16,2]{1,2,0:T(2,128)S(1)} all-to-all(s32[16,16,2]{1,2,0:T(2,128)S(1)} %copy.59), channel_id=1, replica_groups=mesh['pb'=16,'kv'=16] {'pb'}, dimensions={0} | all-to-all | bytes 4096 | tf_op jit(solution)/shard_map/all_to_all | solution.py:51
  26.1 7.3 all-to-all-start.1
  38.5 13.6 %gather_fusion.2 = bf16[512,64,256]{2,1,0:T(8,128)(2,1)} fusion(bf16[32,64,256]{2,1,0:T(8,128)(2,1)S(1)} %pad_maximum_fusion.1, s32[1024]{0:T(1024)S(1)} %pad_clamp_fusion.1), kind=kCustom, calls=%fused_computation.2 | custom fusion | bytes 33556480 | tf_op jit(solution)/shard_map/jit(_take)/gather | solution.py:57
  52.1 8.5 broadcast_select_fusion
  60.6 367.0 %all_to_all.21 = bf16[16,16,2,64,256]{4,3,2,1,0:T(8,128)(2,1)S(1)} all-to-all(bf16[16,16,2,64,256]{4,3,2,1,0:T(8,128)(2,1)S(1)} %broadcast_select_fusion), channel_id=1, replica_groups=mesh['pb'=16,'kv'=16] {'pb'}, dimensions={0} | all-to-all | bytes 33554432 | tf_op jit(solution)/shard_map/all_to_all | solution.py:61
  427.6 6.7 copy.63
  434.3 8.4 all-to-all-start.3
  446.8 4.1 reshape.149
  450.9 240.5 %all-to-all-done.3 = bf16[16,16,2,64,256]{4,3,2,0,1:T(8,128)(2,1)} async-done(((bf16[16,16,2,64,256]{4,3,2,0,1:T(8,128)(2,1)}), bf16[16,16,2,64,256]{4,3,2,0,1:T(8,128)(2,1)}, u32[]{:S(2)}, u32[]{:S(2)}) %all-to-all-start.3) | async-done | bytes 16777248 | tf_op jit(solution)/shard_map/all_to_all | solution.py:60
  691.4 14.2 %copy.64 = bf16[16,16,2,64,256]{4,3,2,1,0:T(8,128)(2,1)} copy(bf16[16,16,2,64,256]{4,3,2,0,1:T(8,128)(2,1)} %all-to-all-done.3) | data formatting | bytes 33554432 | tf_op jit(solution)/shard_map/all_to_all | solution.py:60
  705.5 128.7 %all-reduce.3.cloned.1.call-done = (bf16[1,64,256]{2,1,0:T(8,128)(2,1)}, bf16[1,64,256]{2,1,0:T(8,128)(2,1)}) async-done(((bf16[1,64,256]{2,1,0:T(8,128)(2,1)}, bf16[1,64,256]{2,1,0:T(8,128)(2,1)}), (bf16[1,64,256]{2,1,0:T(8,128)(2,1)}, bf16[1,64,256]{2,1,0:T(8,128)(2,1)})) %all-reduce.3.cloned.1.call-update) | async-done | bytes 65552 | tf_op jit(solution)/shard_map/psum | solution.py:18
  834.3 14.5 %pad_maximum_fusion = bf16[514,64,256]{2,1,0:T(8,128)(2,1)} fusion(bf16[1,64,256]{2,1,0:T(8,128)(2,1)} %get-tuple-element.43, bf16[1,64,256]{2,1,0:T(8,128)(2,1)} %get-tuple-element.44, bf16[512,64,256]{2,1,0:T(8,128)(2,1)} %bitcast.40), kind=kLoop, calls=%fused_computation.26 | loop fusion | flops 16842752 | bytes 33685504 | tf_op jit(solution)/shard_map/concatenate | solution.py:74
  848.7 71.1 %while.10 = (s32[]{:T(128)}, bf16[3,8,512,128]{3,2,1,0:T(8,128)(2,1)}, bf16[3,8,512,128]{3,2,1,0:T(8,128)(2,1)S(1)}, s32[3,8,16]{2,1,0:T(8,128)S(1)}, bf16[514,64,256]{2,1,0:T(8,128)(2,1)}, /*index=5*/s32[]{:T(128)}) while((s32[]{:T(128)}, bf16[3,8,512,128]{3,2,1,0:T(8,128)(2,1)}, bf16[3,8,512,128]{3,2,1,0:T(8,128)(2,1)S(1)}, ...), condition=%wide.region_8.9_spmd, body=%wide.region_5.8_spmd.sunk | while | flops 2184177664 | bytes 73524040 | solution.py:102
  848.8 8.6 gather_fusion
  857.6 4.6 bitcast_select_fusion.2
  864.6 3.5 fusion.40
  868.2 4.3 bitcast_dynamic-update-slice_fusion.2
  872.5 8.6 gather_fusion
  881.3 4.6 bitcast_select_fusion.2
  891.9 4.3 bitcast_dynamic-update-slice_fusion.2
  896.2 8.6 gather_fusion
  905.0 4.6 bitcast_select_fusion.2
  915.6 4.3 bitcast_dynamic-update-slice_fusion.2
  919.9 5.8 reshape.156
  (63 shorter events, 27.6 us)
Async XLA Ops:
  26.1 11.8 %all-to-all-start.1 = ((s32[16,16,2]{0,2,1:T(2,128)}), s32[16,16,2]{0,2,1:T(2,128)S(1)}, u32[]{:S(2)}, u32[]{:S(2)}) async-start(s32[16,16,2]{0,2,1:T(2,128)} %copy.60), calls=%async_computation.1 | async-start | bytes 32768 | tf_op jit(solution)/shard_map/all_to_all | solution.py:50
  434.3 8.7 copy-start
  434.3 8.7 copy-start.1
  434.3 257.1 %all-to-all-start.3 = ((bf16[16,16,2,64,256]{4,3,2,0,1:T(8,128)(2,1)}), bf16[16,16,2,64,256]{4,3,2,0,1:T(8,128)(2,1)}, u32[]{:S(2)}, u32[]{:S(2)}) async-start(bf16[16,16,2,64,256]{4,3,2,0,1:T(8,128)(2,1)} %copy.63), calls=%async_computation.3 | async-start | bytes 33554432 | tf_op jit(solution)/shard_map/all_to_all | solution.py:60
  442.7 3.9 copy-start.2
  442.7 391.5 %all-reduce.3.cloned.1.call-start = ((), (), s32[]{:S(2)}) async-start(), calls=%async_computation.4 | async-start | bytes 131072 | tf_op jit(solution)/shard_map/psum | solution.py:18
Sparse Core Ops, SparseCore 0:
  449.3 384.9 all-reduce.2
where the time goes:
time: 936 us; the launch traced here: 932 us
  blocking collectives  383 us (41%)
  waiting for transfers between devices  372 us (40%)
  local copies, waits for them, and re-layouts  76.1 us (8%)
  other arithmetic  51.3 us (5%)
  matrix products  20 us (2%)
  starting transfers between devices  16 us (2%)
  between operations  13.6 us (1%)
    all_to_all x1, blocking collectives, per_device(): lax.all_to_all(outgoing, 'pb', split_axis=0, concat_axis=0, tiled=True)  367 us
    all_to_all x1, waiting for transfers between devices, per_device(): lax.all_to_all(lax.all_to_all(outgoing, 'pb', split_axis=0, concat_axis=0...  240 us
    psum x1, waiting for transfers between devices, broadcast(): return lax.psum(jnp.where(mine, value, jnp.zeros_like(value)), axis)  129 us
    gather x3, local copies, waits for them, and re-layouts, attend(): jnp.take(tile_table, positions_in.reshape(-1), axis=0)  25.8 us
  transfers between devices with their start and end apart: 3, of which 3 were waited for; matrix products, arithmetic and copies ran while one was open for 2% of the time, Pallas kernels for 0%

commit v1 on v0

--- a/solution.py
+++ b/solution.py
@@ -11,11 +11,6 @@
 TOPN = 16
 QB = 64
 CAP = 2
-
-
-def broadcast(value, axis, root):
-    mine = lax.axis_index(axis) == root
-    return lax.psum(jnp.where(mine, value, jnp.zeros_like(value)), axis)
 
 
 def holdings(wanted, owner, blocks_here):
@@ -38,40 +33,35 @@
     devices = pb_count * kv_count
     blocks_here = keys.shape[0] // BLOCK
     query_blocks = queries.shape[0] // QB
+    column_blocks = pb_count * blocks_here
     tiles_local = jnp.concatenate(
         [keys.reshape(blocks_here, BLOCK, DH), values.reshape(blocks_here, BLOCK, DH)], axis=2
     )
+    column = lax.all_gather(tiles_local, "pb", axis=0, tiled=True)
     slots = CAP
     wanted = selected.reshape(-1)
     owners = jnp.arange(devices, dtype=jnp.int32)
     present, slot_rank = jax.vmap(lambda owner: holdings(wanted, owner, blocks_here))(owners)
     owner_lists = slot_lists(present, slot_rank, slots)
-    by_axes = owner_lists.reshape(kv_count, pb_count, slots).transpose(1, 0, 2)
-    asked_for = lax.all_to_all(
-        lax.all_to_all(by_axes, "pb", split_axis=0, concat_axis=0, tiled=True),
-        "kv",
-        split_axis=1,
-        concat_axis=1,
-        tiled=True,
+    by_column = owner_lists.reshape(kv_count, pb_count, slots) + (
+        jnp.arange(pb_count, dtype=jnp.int32)[None, :, None] * blocks_here
     )
-    outgoing = jnp.take(tiles_local, asked_for.reshape(-1), axis=0).reshape(
-        pb_count, kv_count, slots, BLOCK, 2 * DH
+    by_column = by_column.reshape(kv_count, pb_count * slots)
+    asked_for = lax.all_to_all(by_column, "kv", split_axis=0, concat_axis=0, tiled=True)
+    outgoing = jnp.take(column, asked_for.reshape(-1), axis=0).reshape(
+        kv_count, pb_count * slots, BLOCK, 2 * DH
     )
-    fetched = lax.all_to_all(
-        lax.all_to_all(outgoing, "pb", split_axis=0, concat_axis=0, tiled=True),
-        "kv",
-        split_axis=1,
-        concat_axis=1,
-        tiled=True,
-    )
+    fetched = lax.all_to_all(outgoing, "kv", split_axis=0, concat_axis=0, tiled=True)
     tile_table = fetched.reshape(devices * slots, BLOCK, 2 * DH)
     owner_of = selected // blocks_here
-    positions = (owner_of % pb_count * kv_count + owner_of // pb_count) * slots + jnp.take(
-        slot_rank.reshape(-1), selected
+    positions = owner_of * slots + jnp.take(slot_rank.reshape(-1), selected)
+    me_kv = lax.axis_index("kv")
+    ends = jnp.concatenate([column[:1], column[column_blocks - 1 :]], axis=0)
+    ends = jnp.where(
+        jnp.stack([me_kv == 0, me_kv == kv_count - 1])[:, None, None], ends, jnp.zeros_like(ends)
     )
-    first_tile = broadcast(tiles_local[:1], ("pb", "kv"), 0)
-    latest = broadcast(tiles_local[blocks_here - 1 :], ("pb", "kv"), devices - 1)
-    tile_table = jnp.concatenate([tile_table, first_tile, latest], axis=0)
+    ends = lax.psum(ends, "kv")
+    tile_table = jnp.concatenate([tile_table, ends], axis=0)
     extra_base = devices * slots
     leading_positions = jnp.broadcast_to(
         jnp.array([extra_base, extra_base + 1], jnp.int32), (query_blocks, 2)

time: 936 us -> 521 us (0.56)
  blocking collectives: 383 us -> 11.5 us
  waiting for transfers between devices: 372 us -> 346 us
  local copies, waits for them, and re-layouts: 76.1 us -> 61.4 us
    all_to_all x2 -> x1, blocking collectives: 383 us -> 11.5 us  [per_device(): lax.all_to_all(by_column, 'kv', split_axis=0, concat_axis=0, tiled=True)]
    all_to_all x2 -> x1, waiting for transfers between devices: 244 us -> 0.01 us  [per_device(): lax.all_to_all(outgoing, 'kv', split_axis=0, concat_axis=0, tiled=True)]
    psum x1, waiting for transfers between devices: 129 us -> 263 us  [per_device(): ends = lax.psum(ends, 'kv')]
    all_gather x0 -> x1, waiting for transfers between devices: none -> 82.6 us  [per_device(): column = lax.all_gather(tiles_local, 'pb', axis=0, tiled=True)]
    all_to_all x4 -> x1, local copies, waits for them, and re-layouts: 21.7 us -> 0.51 us  [per_device(): lax.all_to_all(by_column, 'kv', split_axis=0, concat_axis=0, tiled=True)]
  transfers between devices with their start and end apart: 3 -> 3, of which waited for: 3 -> 2; matrix products, arithmetic and copies ran while one was open for 2% -> 3% of each run, Pallas kernels for 0% -> 0%
where the time goes in v1:
time: 521 us; the launch traced here: 518 us
  waiting for transfers between devices  346 us (66%)
  local copies, waits for them, and re-layouts  61.4 us (12%)
  other arithmetic  58.3 us (11%)
  matrix products  20 us (4%)
  between operations  13.6 us (3%)
  blocking collectives  11.5 us (2%)
  starting transfers between devices  7.39 us (1%)
    psum x1, waiting for transfers between devices, per_device(): ends = lax.psum(ends, 'kv')  263 us
    all_gather x1, waiting for transfers between devices, per_device(): column = lax.all_gather(tiles_local, 'pb', axis=0, tiled=True)  82.6 us
    gather x3, local copies, waits for them, and re-layouts, attend(): jnp.take(tile_table, positions_in.reshape(-1), axis=0)  25.6 us
    gather x1, local copies, waits for them, and re-layouts, per_device(): jnp.take(column, asked_for.reshape(-1), axis=0)  19.5 us
    select_n x2, other arithmetic, per_device(): jnp.take(column, asked_for.reshape(-1), axis=0)  14.1 us
    concatenate x1, other arithmetic, per_device(): tile_table = jnp.concatenate([tile_table, ends], axis=0)  14.1 us
    select_n x6, other arithmetic, attend(): jnp.take(tile_table, positions_in.reshape(-1), axis=0)  13.7 us
    dot_general x3, matrix products, attend(): jnp.einsum('gqk,gkd->gqd', weights.astype(jnp.bfloat16), gathered[..., DH...  12.7 us
  transfers between devices with their start and end apart: 3, of which 2 were waited for; matrix products, arithmetic and copies ran while one was open for 3% of the time, Pallas kernels for 0%

profile of v1, /device:TPU:12, one launch (start us, length us, event | category | flops | bytes accessed | tf_op | source)
XLA Modules:
  0.0 517.8 jit_solution(11960891043452149832)
XLA Ops:
  12.1 11.5 %all_to_all.11 = s32[16,1,32]{2,1,0:T(1,128)S(1)} all-to-all(s32[16,1,32]{2,1,0:T(1,128)S(1)} %bitcast.44), channel_id=1, replica_groups=mesh['pb'=16,'kv'=16] {'kv'}, dimensions={0} | all-to-all | bytes 4096 | tf_op jit(solution)/shard_map/all_to_all | solution.py:50
  24.8 82.6 %all-gather.2.cloned.1.call-done = bf16[512,64,256]{2,1,0:T(8,128)(2,1)} async-done(((bf16[32,64,256]{2,1,0:T(8,128)(2,1)}), bf16[512,64,256]{2,1,0:T(8,128)(2,1)}) %all-gather.2.cloned.1.call-update) | async-done | bytes 16777232 | tf_op jit(solution)/shard_map/all_gather | solution.py:40
  107.5 19.5 %gather_fusion.2 = bf16[512,64,256]{2,1,0:T(8,128)(2,1)} fusion(bf16[512,64,256]{2,1,0:T(8,128)(2,1)} %all-gather.2.cloned.1.call-done, s32[1024]{0:T(1024)S(1)} %pad_clamp_fusion.1), kind=kCustom, calls=%fused_computation.2 | custom fusion | bytes 33556480 | tf_op jit(solution)/shard_map/jit(_take)/gather | solution.py:51
  127.0 14.1 %broadcast_select_fusion = bf16[16,32,64,256]{3,2,1,0:T(8,128)(2,1)} fusion(bf16[16,32,64,256]{3,2,1,0:T(8,128)(2,1)} %bitcast.40, pred[16,32]{1,0:T(8,128)(4,1)S(1)} %compare_and_fusion.1), kind=kLoop, calls=%fused_computation.27 | loop fusion | flops 8388608 | bytes 33554944 | tf_op jit(solution)/shard_map/jit(_take)/select_n | solution.py:51
  141.1 7.4 %all-to-all-start.1 = ((bf16[16,32,64,256]{3,2,1,0:T(8,128)(2,1)}), bf16[16,32,64,256]{3,2,1,0:T(8,128)(2,1)}, u32[]{:S(2)}, u32[]{:S(2)}) async-start(bf16[16,32,64,256]{3,2,1,0:T(8,128)(2,1)} %broadcast_select_fusion), calls=%async_computation.1 | async-start | bytes 33554432 | tf_op jit(solution)/shard_map/all_to_all | solution.py:54
  148.9 2.5 gather_fusion.1
  153.2 4.1 reshape.203
  157.3 262.9 %all-reduce.2.cloned.1.call-done = bf16[2,64,256]{2,1,0:T(8,128)(2,1)} async-done(((bf16[2,64,256]{2,1,0:T(8,128)(2,1)}), bf16[2,64,256]{2,1,0:T(8,128)(2,1)}) %all-reduce.2.cloned.1.call-update) | async-done | bytes 65552 | tf_op jit(solution)/shard_map/psum | solution.py:63
  420.2 14.1 %pad_maximum_fusion = bf16[514,64,256]{2,1,0:T(8,128)(2,1)} fusion(bf16[2,64,256]{2,1,0:T(8,128)(2,1)} %all-reduce.2.cloned.1.call-done, bf16[512,64,256]{2,1,0:T(8,128)(2,1)} %bitcast.12), kind=kLoop, calls=%fused_computation.26 | loop fusion | flops 8421376 | bytes 33685504 | tf_op jit(solution)/shard_map/concatenate | solution.py:64
  434.3 70.9 %while.10 = (s32[]{:T(128)}, bf16[3,8,512,128]{3,2,1,0:T(8,128)(2,1)}, bf16[3,8,512,128]{3,2,1,0:T(8,128)(2,1)S(1)}, s32[3,8,16]{2,1,0:T(8,128)S(1)}, bf16[514,64,256]{2,1,0:T(8,128)(2,1)}, /*index=5*/s32[]{:T(128)}) while((s32[]{:T(128)}, bf16[3,8,512,128]{3,2,1,0:T(8,128)(2,1)}, bf16[3,8,512,128]{3,2,1,0:T(8,128)(2,1)S(1)}, ...), condition=%wide.region_7.8_spmd, body=%wide.region_4.7_spmd.sunk | while | flops 2184177664 | bytes 73523544 | solution.py:92
  434.6 8.5 %gather_fusion = bf16[128,64,256]{2,1,0:T(8,128)(2,1)} fusion(bf16[514,64,256]{2,1,0:T(8,128)(2,1)} %get-tuple-element.104, s32[1024]{0:T(1024)S(1)} %pad_clamp_fusion.4), kind=kCustom, calls=%fused_computation.clone.1 | custom fusion | bytes 8389120 | tf_op jit(solution)/shard_map/while/body/eval_jaxpr/jit(_take)/gather | solution.py:76
  443.2 4.6 bitcast_select_fusion.2
  450.1 3.5 fusion.31
  453.7 4.2 bitcast_dynamic-update-slice_fusion.2
  458.2 8.5 %gather_fusion = bf16[128,64,256]{2,1,0:T(8,128)(2,1)} fusion(bf16[514,64,256]{2,1,0:T(8,128)(2,1)} %get-tuple-element.104, s32[1024]{0:T(1024)S(1)} %pad_clamp_fusion.4), kind=kCustom, calls=%fused_computation.clone.1 | custom fusion | bytes 8389120 | tf_op jit(solution)/shard_map/while/body/eval_jaxpr/jit(_take)/gather | solution.py:76
  466.8 4.6 bitcast_select_fusion.2
  473.8 3.5 fusion.31
  477.3 4.2 bitcast_dynamic-update-slice_fusion.2
  481.9 8.5 %gather_fusion = bf16[128,64,256]{2,1,0:T(8,128)(2,1)} fusion(bf16[514,64,256]{2,1,0:T(8,128)(2,1)} %get-tuple-element.104, s32[1024]{0:T(1024)S(1)} %pad_clamp_fusion.4), kind=kCustom, calls=%fused_computation.clone.1 | custom fusion | bytes 8389120 | tf_op jit(solution)/shard_map/while/body/eval_jaxpr/jit(_take)/gather | solution.py:76
  490.4 4.6 bitcast_select_fusion.2
  495.0 2.4 multiply_reduce_fusion.2
  497.4 3.5 fusion.31
  500.9 4.2 bitcast_dynamic-update-slice_fusion.2
  505.2 5.8 %reshape.211 = bf16[1536,1024]{1,0:T(8,128)(2,1)} reshape(bf16[3,8,512,128]{3,2,1,0:T(8,128)(2,1)} %get-tuple-element.32) | data formatting | bytes 6291456 | tf_op jit(solution)/shard_map/reshape | solution.py:93
  (62 shorter events, 14.4 us)
Async XLA Ops:
  6.5 100.9 %all-gather.2.cloned.1.call-start = ((), (), s32[]{:S(2)}) async-start(), calls=%async_computation.2 | async-start | bytes 17825792 | tf_op jit(solution)/shard_map/all_gather | solution.py:40
  141.1 7.5 %copy-start = (s32[2]{0:T(128)S(1)}, s32[2]{0:T(128)}, u32[]{:S(2)}) copy-start(s32[2]{0:T(128)} %constant.100.clone) | copy-start | bytes 28
  141.1 279.1 %all-to-all-start.1 = ((bf16[16,32,64,256]{3,2,1,0:T(8,128)(2,1)}), bf16[16,32,64,256]{3,2,1,0:T(8,128)(2,1)}, u32[]{:S(2)}, u32[]{:S(2)}) async-start(bf16[16,32,64,256]{3,2,1,0:T(8,128)(2,1)} %broadcast_select_fusion), calls=%async_computation.1 | async-start | bytes 33554432 | tf_op jit(solution)/shard_map/all_to_all | solution.py:54
  148.5 271.8 %all-reduce.2.cloned.1.call-start = ((), (), s32[]{:S(2)}) async-start(), calls=%async_computation.3 | async-start | bytes 131072 | tf_op jit(solution)/shard_map/psum | solution.py:63
Sparse Core Ops, SparseCore 0:
  9.2 98.2 all-gather.1
  153.2 266.9 all-reduce.1

commit v2 on v1

--- a/solution.py
+++ b/solution.py
@@ -48,23 +48,22 @@
     )
     by_column = by_column.reshape(kv_count, pb_count * slots)
     asked_for = lax.all_to_all(by_column, "kv", split_axis=0, concat_axis=0, tiled=True)
-    outgoing = jnp.take(column, asked_for.reshape(-1), axis=0).reshape(
-        kv_count, pb_count * slots, BLOCK, 2 * DH
+    me_kv = lax.axis_index("kv")
+    end_pick = jnp.where(me_kv == kv_count - 1, column_blocks - 1, 0).astype(jnp.int32)
+    picks = jnp.concatenate(
+        [asked_for.reshape(kv_count, pb_count * slots), jnp.broadcast_to(end_pick, (kv_count, 1))], axis=1
+    )
+    outgoing = jnp.take(column, picks.reshape(-1), axis=0).reshape(
+        kv_count, pb_count * slots + 1, BLOCK, 2 * DH
     )
     fetched = lax.all_to_all(outgoing, "kv", split_axis=0, concat_axis=0, tiled=True)
-    tile_table = fetched.reshape(devices * slots, BLOCK, 2 * DH)
+    tile_table = fetched.reshape(devices * slots + kv_count, BLOCK, 2 * DH)
     owner_of = selected // blocks_here
     positions = owner_of * slots + jnp.take(slot_rank.reshape(-1), selected)
-    me_kv = lax.axis_index("kv")
-    ends = jnp.concatenate([column[:1], column[column_blocks - 1 :]], axis=0)
-    ends = jnp.where(
-        jnp.stack([me_kv == 0, me_kv == kv_count - 1])[:, None, None], ends, jnp.zeros_like(ends)
-    )
-    ends = lax.psum(ends, "kv")
-    tile_table = jnp.concatenate([tile_table, ends], axis=0)
-    extra_base = devices * slots
+    positions = positions + owner_of // pb_count
+    row = pb_count * slots + 1
     leading_positions = jnp.broadcast_to(
-        jnp.array([extra_base, extra_base + 1], jnp.int32), (query_blocks, 2)
+        jnp.array([row - 1, kv_count * row - 1], jnp.int32), (query_blocks, 2)
     )
     positions = jnp.concatenate([leading_positions, positions], axis=1)
     group_size = math.gcd(query_blocks, 8)

time: 521 us -> 495 us (0.950)
  other arithmetic: 58.3 us -> 43.8 us
  waiting for transfers between devices: 346 us -> 334 us
  blocking collectives: 11.5 us -> 0 us
  starting transfers between devices: 7.39 us -> 14.6 us
    psum x1 -> x0, waiting for transfers between devices: 263 us -> none  [per_device(): ends = lax.psum(ends, 'kv')]
    all_to_all x1, waiting for transfers between devices: 0.01 us -> 247 us  [per_device(): lax.all_to_all(outgoing, 'kv', split_axis=0, concat_axis=0, tiled=True)]
    concatenate x1 -> x0, other arithmetic: 14.1 us -> none  [per_device(): tile_table = jnp.concatenate([tile_table, ends], axis=0)]
    all_to_all x1 -> x0, blocking collectives: 11.5 us -> none  [per_device(): lax.all_to_all(by_column, 'kv', split_axis=0, concat_axis=0, tiled=True)]
    all_to_all x0 -> x1, starting transfers between devices: none -> 7.34 us  [per_device(): lax.all_to_all(by_column, 'kv', split_axis=0, concat_axis=0, tiled=True)]
    select_n x3 -> x2, other arithmetic: 14.8 us -> 14.5 us  [per_device(): jnp.take(column, picks.reshape(-1), axis=0)]
  transfers between devices with their start and end apart: 3 -> 3, of which waited for: 2 -> 3; matrix products, arithmetic and copies ran while one was open for 3% -> 2% of each run, Pallas kernels for 0% -> 0%
where the time goes in v2:
time: 495 us; the launch traced here: 489 us
  waiting for transfers between devices  334 us (67%)
  local copies, waits for them, and re-layouts  62.3 us (13%)
  other arithmetic  43.8 us (9%)
  matrix products  20 us (4%)
  starting transfers between devices  14.6 us (3%)
  between operations  13.6 us (3%)
    all_to_all x1, waiting for transfers between devices, per_device(): lax.all_to_all(outgoing, 'kv', split_axis=0, concat_axis=0, tiled=True)  247 us
    all_gather x1, waiting for transfers between devices, per_device(): column = lax.all_gather(tiles_local, 'pb', axis=0, tiled=True)  82.9 us
    gather x3, local copies, waits for them, and re-layouts, attend(): jnp.take(tile_table, positions_in.reshape(-1), axis=0)  26.1 us
    gather x1, local copies, waits for them, and re-layouts, per_device(): jnp.take(column, picks.reshape(-1), axis=0)  21.2 us
    select_n x2, other arithmetic, per_device(): jnp.take(column, picks.reshape(-1), axis=0)  14.5 us
    select_n x6, other arithmetic, attend(): jnp.take(tile_table, positions_in.reshape(-1), axis=0)  13.8 us
    dot_general x3, matrix products, attend(): jnp.einsum('gqk,gkd->gqd', weights.astype(jnp.bfloat16), gathered[..., DH...  12.7 us
    reduce_sum x3, other arithmetic, attend(): totals = jnp.sum(weights, axis=-1, keepdims=True)  10.6 us
  transfers between devices with their start and end apart: 3, of which 3 were waited for; matrix products, arithmetic and copies ran while one was open for 2% of the time, Pallas kernels for 0%

profile of v2, /device:TPU:12, one launch (start us, length us, event | category | flops | bytes accessed | tf_op | source)
XLA Modules:
  0.0 488.5 jit_solution(9905077446433948110)
XLA Ops:
  12.7 7.3 %all-to-all-start = ((s32[16,1,32]{2,1,0:T(1,128)}), s32[16,1,32]{2,1,0:T(1,128)S(1)}, u32[]{:S(2)}, u32[]{:S(2)}) async-start(s32[16,1,32]{2,1,0:T(1,128)} %bitcast.6), calls=%async_computation | async-start | bytes 16384 | tf_op jit(solution)/shard_map/all_to_all | solution.py:50
  20.0 4.4 all-to-all-done
  24.6 82.9 %all-gather.2.cloned.1.call-done = bf16[512,64,256]{2,1,0:T(8,128)(2,1)} async-done(((bf16[32,64,256]{2,1,0:T(8,128)(2,1)}), bf16[512,64,256]{2,1,0:T(8,128)(2,1)}) %all-gather.2.cloned.1.call-update) | async-done | bytes 16777232 | tf_op jit(solution)/shard_map/all_gather | solution.py:40
  107.5 21.2 %gather_fusion.2 = bf16[528,64,256]{2,1,0:T(8,128)(2,1)} fusion(bf16[512,64,256]{2,1,0:T(8,128)(2,1)} %all-gather.2.cloned.1.call-done, s32[1024]{0:T(1024)S(1)} %pad_clamp_fusion.1), kind=kCustom, calls=%fused_computation.2 | custom fusion | bytes 34605120 | tf_op jit(solution)/shard_map/jit(_take)/gather | solution.py:56
  128.7 14.4 %broadcast_select_fusion = bf16[16,33,64,256]{3,2,1,0:T(8,128)(2,1)} fusion(bf16[16,33,64,256]{3,2,1,0:T(8,128)(2,1)} %bitcast.37, pred[16,33]{1,0:T(8,128)(4,1)S(1)} %compare_and_fusion.1), kind=kLoop, calls=%fused_computation.26 | loop fusion | flops 8650752 | bytes 34603536 | tf_op jit(solution)/shard_map/jit(_take)/select_n | solution.py:56
  143.1 7.2 %all-to-all-start.1 = ((bf16[16,33,64,256]{3,2,1,0:T(8,128)(2,1)}), bf16[16,33,64,256]{3,2,1,0:T(8,128)(2,1)}, u32[]{:S(2)}, u32[]{:S(2)}) async-start(bf16[16,33,64,256]{3,2,1,0:T(8,128)(2,1)} %broadcast_select_fusion), calls=%async_computation.1 | async-start | bytes 34603008 | tf_op jit(solution)/shard_map/all_to_all | solution.py:59
  150.7 2.5 gather_fusion.1
  153.4 4.1 reshape.197
  157.6 246.9 %all-to-all-done.1 = bf16[16,33,64,256]{3,2,1,0:T(8,128)(2,1)} async-done(((bf16[16,33,64,256]{3,2,1,0:T(8,128)(2,1)}), bf16[16,33,64,256]{3,2,1,0:T(8,128)(2,1)}, u32[]{:S(2)}, u32[]{:S(2)}) %all-to-all-start.1) | async-done | bytes 17301536 | tf_op jit(solution)/shard_map/all_to_all | solution.py:59
  404.5 71.4 %while.10 = (s32[]{:T(128)}, bf16[3,8,512,128]{3,2,1,0:T(8,128)(2,1)}, bf16[3,8,512,128]{3,2,1,0:T(8,128)(2,1)S(1)}, s32[3,8,16]{2,1,0:T(8,128)S(1)}, bf16[528,64,256]{2,1,0:T(8,128)(2,1)}, /*index=5*/s32[]{:T(128)}) while((s32[]{:T(128)}, bf16[3,8,512,128]{3,2,1,0:T(8,128)(2,1)}, bf16[3,8,512,128]{3,2,1,0:T(8,128)(2,1)S(1)}, ...), condition=%wide.region_6.7_spmd, body=%wide.region_3.6_spmd.sunk | while | flops 2184177664 | bytes 73524040 | solution.py:91
  404.6 8.7 %gather_fusion = bf16[128,64,256]{2,1,0:T(8,128)(2,1)} fusion(bf16[528,64,256]{2,1,0:T(8,128)(2,1)} %get-tuple-element.102, s32[1024]{0:T(1024)S(1)} %pad_clamp_fusion.4), kind=kCustom, calls=%fused_computation.clone.1 | custom fusion | bytes 8389120 | tf_op jit(solution)/shard_map/while/body/eval_jaxpr/jit(_take)/gather | solution.py:75
  413.5 4.6 bitcast_select_fusion.2
  418.1 2.4 multiply_reduce_fusion.2
  420.5 3.5 fusion.32
  424.1 4.3 bitcast_dynamic-update-slice_fusion.2
  428.4 8.7 %gather_fusion = bf16[128,64,256]{2,1,0:T(8,128)(2,1)} fusion(bf16[528,64,256]{2,1,0:T(8,128)(2,1)} %get-tuple-element.102, s32[1024]{0:T(1024)S(1)} %pad_clamp_fusion.4), kind=kCustom, calls=%fused_computation.clone.1 | custom fusion | bytes 8389120 | tf_op jit(solution)/shard_map/while/body/eval_jaxpr/jit(_take)/gather | solution.py:75
  437.3 4.6 bitcast_select_fusion.2
  444.3 3.5 fusion.32
  447.9 4.2 bitcast_dynamic-update-slice_fusion.2
  452.2 8.7 %gather_fusion = bf16[128,64,256]{2,1,0:T(8,128)(2,1)} fusion(bf16[528,64,256]{2,1,0:T(8,128)(2,1)} %get-tuple-element.102, s32[1024]{0:T(1024)S(1)} %pad_clamp_fusion.4), kind=kCustom, calls=%fused_computation.clone.1 | custom fusion | bytes 8389120 | tf_op jit(solution)/shard_map/while/body/eval_jaxpr/jit(_take)/gather | solution.py:75
  461.1 4.6 bitcast_select_fusion.2
  468.1 3.5 fusion.32
  471.7 4.2 bitcast_dynamic-update-slice_fusion.2
  475.9 5.8 %reshape.204 = bf16[1536,1024]{1,0:T(8,128)(2,1)} reshape(bf16[3,8,512,128]{3,2,1,0:T(8,128)(2,1)} %get-tuple-element.32) | data formatting | bytes 6291456 | tf_op jit(solution)/shard_map/reshape | solution.py:92
  (55 shorter events, 12.3 us)
Async XLA Ops:
  6.5 100.9 %all-gather.2.cloned.1.call-start = ((), (), s32[]{:S(2)}) async-start(), calls=%async_computation.2 | async-start | bytes 17825792 | tf_op jit(solution)/shard_map/all_gather | solution.py:40
  12.7 11.7 %all-to-all-start = ((s32[16,1,32]{2,1,0:T(1,128)}), s32[16,1,32]{2,1,0:T(1,128)S(1)}, u32[]{:S(2)}, u32[]{:S(2)}) async-start(s32[16,1,32]{2,1,0:T(1,128)} %bitcast.6), calls=%async_computation | async-start | bytes 16384 | tf_op jit(solution)/shard_map/all_to_all | solution.py:50
  143.1 261.4 %all-to-all-start.1 = ((bf16[16,33,64,256]{3,2,1,0:T(8,128)(2,1)}), bf16[16,33,64,256]{3,2,1,0:T(8,128)(2,1)}, u32[]{:S(2)}, u32[]{:S(2)}) async-start(bf16[16,33,64,256]{3,2,1,0:T(8,128)(2,1)} %broadcast_select_fusion), calls=%async_computation.1 | async-start | bytes 34603008 | tf_op jit(solution)/shard_map/all_to_all | solution.py:59
  150.7 2.7 copy-start
Sparse Core Ops, SparseCore 0:
  9.2 98.2 all-gather.1

commit v3 on v2

--- a/solution.py
+++ b/solution.py
@@ -3,6 +3,8 @@
 import jax
 import jax.numpy as jnp
 from jax import lax
+from jax.experimental import pallas as pl
+from jax.experimental.pallas import tpu as pltpu
 from jax.sharding import PartitionSpec as P
 
 H = 8
@@ -53,7 +55,7 @@
     picks = jnp.concatenate(
         [asked_for.reshape(kv_count, pb_count * slots), jnp.broadcast_to(end_pick, (kv_count, 1))], axis=1
     )
-    outgoing = jnp.take(column, picks.reshape(-1), axis=0).reshape(
+    outgoing = jnp.take(column, picks.reshape(-1), axis=0, mode="clip").reshape(
         kv_count, pb_count * slots + 1, BLOCK, 2 * DH
     )
     fetched = lax.all_to_all(outgoing, "kv", split_axis=0, concat_axis=0, tiled=True)
@@ -66,30 +68,79 @@
         jnp.array([row - 1, kv_count * row - 1], jnp.int32), (query_blocks, 2)
     )
     positions = jnp.concatenate([leading_positions, positions], axis=1)
-    group_size = math.gcd(query_blocks, 8)
-    q_groups = queries.reshape(query_blocks // group_size, group_size, QB * H, DH)
-    p_groups = positions.reshape(query_blocks // group_size, group_size, TOPN)
+    positions = jnp.clip(positions, 0, tile_table.shape[0] - 1).reshape(-1)
+    return attend_blocks(queries, tile_table, positions)
 
-    def attend(operands):
-        q_block, positions_in = operands
-        gathered = jnp.take(tile_table, positions_in.reshape(-1), axis=0).reshape(
-            group_size, TOPN * BLOCK, 2 * DH
-        )
-        scores = jnp.einsum(
-            "gqd,gkd->gqk", q_block, gathered[..., :DH], preferred_element_type=jnp.float32
+
+HEAD_GROUP = 4
+
+
+def attend_kernel(pos_ref, q_ref, table_hbm, o_ref, kvbuf, sems):
+    step = pl.program_id(0)
+    steps = pl.num_programs(0)
+
+    def fetch(block, slot):
+        for j in range(TOPN):
+            pltpu.make_async_copy(
+                table_hbm.at[pos_ref[block * TOPN + j]], kvbuf.at[slot, j], sems.at[slot, j]
+            ).start()
+
+    @pl.when(step == 0)
+    def _():
+        fetch(0, 0)
+
+    slot = step % 2
+
+    @pl.when(step + 1 < steps)
+    def _():
+        fetch(step + 1, 1 - slot)
+
+    for j in range(TOPN):
+        pltpu.make_async_copy(table_hbm.at[0], kvbuf.at[slot, j], sems.at[slot, j]).wait()
+    tiles = kvbuf[slot]
+    k_rows = tiles[:, :, :DH].reshape(TOPN * BLOCK, DH)
+    v_rows = tiles[:, :, DH:].reshape(TOPN * BLOCK, DH)
+    for g in range(H // HEAD_GROUP):
+        heads = range(g * HEAD_GROUP, (g + 1) * HEAD_GROUP)
+        q_rows = jnp.concatenate([q_ref[:, h * DH : (h + 1) * DH] for h in heads], axis=0)
+        scores = lax.dot_general(
+            q_rows, k_rows, (((1,), (1,)), ((), ())), preferred_element_type=jnp.float32
         ) * DH ** (-0.5)
         weights = jnp.exp(scores - jnp.max(scores, axis=-1, keepdims=True))
         totals = jnp.sum(weights, axis=-1, keepdims=True)
-        weighted = jnp.einsum(
-            "gqk,gkd->gqd",
-            weights.astype(jnp.bfloat16),
-            gathered[..., DH:],
-            preferred_element_type=jnp.float32,
+        weighted = jnp.dot(
+            weights.astype(jnp.bfloat16), v_rows, preferred_element_type=jnp.float32
         )
-        return (weighted / totals).astype(jnp.bfloat16)
+        out = (weighted / totals).astype(o_ref.dtype)
+        for i, h in enumerate(heads):
+            o_ref[:, h * DH : (h + 1) * DH] = out[i * QB : (i + 1) * QB]
 
-    result = lax.map(attend, (q_groups, p_groups))
-    return result.reshape(query_blocks * QB, H * DH)
+
+def attend_blocks(queries, tile_table, positions):
+    query_blocks = queries.shape[0] // QB
+    return pl.pallas_call(
+        attend_kernel,
+        out_shape=jax.ShapeDtypeStruct(queries.shape, queries.dtype),
+        grid_spec=pltpu.PrefetchScalarGridSpec(
+            num_scalar_prefetch=1,
+            grid=(query_blocks,),
+            in_specs=[
+                pl.BlockSpec((QB, H * DH), lambda i, pos: (i, 0)),
+                pl.BlockSpec(memory_space=pl.ANY),
+            ],
+            out_specs=pl.BlockSpec((QB, H * DH), lambda i, pos: (i, 0)),
+            scratch_shapes=[
+                pltpu.VMEM((2, TOPN, BLOCK, 2 * DH), tile_table.dtype),
+                pltpu.SemaphoreType.DMA((2, TOPN)),
+            ],
+        ),
+        compiler_params=pltpu.CompilerParams(dimension_semantics=("arbitrary",)),
+        cost_estimate=pl.CostEstimate(
+            flops=4 * queries.shape[0] * H * TOPN * BLOCK * DH,
+            transcendentals=queries.shape[0] * H * TOPN * BLOCK,
+            bytes_accessed=2 * queries.size * 2 + query_blocks * TOPN * BLOCK * 2 * DH * 2,
+        ),
+    )(positions, queries, tile_table)
 
 
 def solution(mesh):

time: 495 us -> 437 us (0.88)
  other arithmetic: 43.8 us -> 4.89 us
  local copies, waits for them, and re-layouts: 62.3 us -> 26.1 us
  Pallas kernels: 0 us -> 34.5 us
  matrix products: 20 us -> 0 us
    pallas_call x0 -> x1, Pallas kernels: none -> 34.5 us  [attend_blocks(): pl.pallas_call(attend_kernel, out_shape=jax.ShapeDtypeStruct(queries.shap...]
    select_n x8 -> x0, other arithmetic: 28.2 us -> none  [the longest x2 14.5 us: per_device(): jnp.take(column, picks.reshape(-1), axis=0)]
    gather x4 -> x1, local copies, waits for them, and re-layouts: 47.3 us -> 21.2 us  [per_device(): jnp.take(column, picks.reshape(-1), axis=0, mode='clip')]
    dot_general x6 -> x0, matrix products: 20 us -> none  [the longest x3 12.7 us: attend(): jnp.einsum('gqk,gkd->gqd', weights.astype(jnp.bfloat16), gathered[..., DH...]
    reduce_sum x3 -> x0, other arithmetic: 10.6 us -> none  [attend(): totals = jnp.sum(weights, axis=-1, keepdims=True)]
    reshape x6 -> x0, local copies, waits for them, and re-layouts: 10.2 us -> none  [the longest x1 5.77 us: per_device(): return result.reshape(query_blocks * QB, H * DH)]
where the time goes in v3:
time: 437 us; the launch traced here: 431 us
  waiting for transfers between devices  338 us (77%)
  Pallas kernels  34.5 us (8%)
  local copies, waits for them, and re-layouts  26.1 us (6%)
  starting transfers between devices  14.6 us (3%)
  between operations  13.6 us (3%)
  other arithmetic  4.89 us (1%)
    all_to_all x1, waiting for transfers between devices, per_device(): lax.all_to_all(outgoing, 'kv', split_axis=0, concat_axis=0, tiled=True)  250 us
    all_gather x1, waiting for transfers between devices, per_device(): column = lax.all_gather(tiles_local, 'pb', axis=0, tiled=True)  83 us
    pallas_call x1, Pallas kernels, attend_blocks(): pl.pallas_call(attend_kernel, out_shape=jax.ShapeDtypeStruct(queries.shap...  34.5 us
    gather x1, local copies, waits for them, and re-layouts, per_device(): jnp.take(column, picks.reshape(-1), axis=0, mode='clip')  21.2 us
  transfers between devices with their start and end apart: 3, of which 3 were waited for; matrix products, arithmetic and copies ran while one was open for 2% of the time, Pallas kernels for 0%

profile of v3, /device:TPU:12, one launch (start us, length us, event | category | flops | bytes accessed | tf_op | source)
XLA Modules:
  0.0 431.5 jit_solution(305004222727450709)
XLA Ops:
  6.5 2.3 pad_maximum_fusion
  8.9 0.1 add.62
  9.0 0.1 add.63
  9.0 0.8 copy.29
  9.8 0.1 eq.42
  9.9 1.7 convert_reduce_fusion
  11.8 0.1 copy.37
  11.9 0.1 reshape.112
  12.1 0.6 broadcast_add_fusion
  12.7 7.3 %all-to-all-start = ((s32[16,1,32]{2,1,0:T(1,128)}), s32[16,1,32]{2,1,0:T(1,128)S(1)}, u32[]{:S(2)}, u32[]{:S(2)}) async-start(s32[16,1,32]{2,1,0:T(1,128)} %bitcast.2), calls=%async_computation | async-start | bytes 16384 | tf_op jit(solution)/shard_map/all_to_all | solution.py:52
  20.0 4.4 %all-to-all-done = s32[16,1,32]{2,1,0:T(1,128)S(1)} async-done(((s32[16,1,32]{2,1,0:T(1,128)}), s32[16,1,32]{2,1,0:T(1,128)S(1)}, u32[]{:S(2)}, u32[]{:S(2)}) %all-to-all-start) | async-done | bytes 2080 | tf_op jit(solution)/shard_map/all_to_all | solution.py:52
  24.4 0.1 reshape.125
  24.5 83.0 %all-gather.2.cloned.1.call-done = bf16[512,64,256]{2,1,0:T(8,128)(2,1)} async-done(((bf16[32,64,256]{2,1,0:T(8,128)(2,1)}), bf16[512,64,256]{2,1,0:T(8,128)(2,1)}) %all-gather.2.cloned.1.call-update) | async-done | bytes 16777232 | tf_op jit(solution)/shard_map/all_gather | solution.py:42
  107.5 21.2 %gather_fusion.1 = bf16[528,64,256]{2,1,0:T(8,128)(2,1)} fusion(bf16[512,64,256]{2,1,0:T(8,128)(2,1)} %all-gather.2.cloned.1.call-done, s32[1024]{0:T(1024)S(1)} %pad_clamp_fusion), kind=kCustom, calls=%fused_computation.1 | custom fusion | bytes 34605120 | tf_op jit(solution)/shard_map/jit(_take)/gather | solution.py:58
  128.7 7.3 %all-to-all-start.1 = ((bf16[16,33,64,256]{3,2,1,0:T(8,128)(2,1)}), bf16[16,33,64,256]{3,2,1,0:T(8,128)(2,1)}, u32[]{:S(2)}, u32[]{:S(2)}) async-start(bf16[16,33,64,256]{3,2,1,0:T(8,128)(2,1)} %bitcast.6), calls=%async_computation.1 | async-start | bytes 34603008 | tf_op jit(solution)/shard_map/all_to_all | solution.py:61
  136.0 0.1 copy.36
  136.1 0.1 reshape.117
  136.2 0.1 sub.23
  136.3 2.5 gather_fusion
  138.9 0.1 reshape.116
  139.0 0.1 add_clamp_fusion
  139.1 0.6 min.12.pos_ref
  139.7 250.4 %all-to-all-done.1 = bf16[16,33,64,256]{3,2,1,0:T(8,128)(2,1)} async-done(((bf16[16,33,64,256]{3,2,1,0:T(8,128)(2,1)}), bf16[16,33,64,256]{3,2,1,0:T(8,128)(2,1)}, u32[]{:S(2)}, u32[]{:S(2)}) %all-to-all-start.1) | async-done | bytes 17301536 | tf_op jit(solution)/shard_map/all_to_all | solution.py:61
  390.1 34.5 %shard_map.55 = bf16[1536,1024]{1,0:T(8,128)(2,1)} custom-call(s32[384]{0:T(512)} %min.12.pos_ref, bf16[1536,1024]{1,0:T(8,128)(2,1)} %q_ref.1, bf16[528,64,256]{2,1,0:T(8,128)(2,1)} %bitcast.5.table_hbm), custom_call_target="tpu_custom_call" | custom-call | flops 6442450944 | bytes 18874368 | tf_op jit(solution)/shard_map/pallas_call | solution.py:121
  (17 shorter events, 0.2 us)
Async XLA Ops:
  6.5 100.9 %all-gather.2.cloned.1.call-start = ((), (), s32[]{:S(2)}) async-start(), calls=%async_computation.2 | async-start | bytes 17825792 | tf_op jit(solution)/shard_map/all_gather | solution.py:42
  12.7 11.7 %all-to-all-start = ((s32[16,1,32]{2,1,0:T(1,128)}), s32[16,1,32]{2,1,0:T(1,128)S(1)}, u32[]{:S(2)}, u32[]{:S(2)}) async-start(s32[16,1,32]{2,1,0:T(1,128)} %bitcast.2), calls=%async_computation | async-start | bytes 16384 | tf_op jit(solution)/shard_map/all_to_all | solution.py:52
  128.7 7.4 %copy-start = (s32[2]{0:T(128)S(1)}, s32[2]{0:T(128)}, u32[]{:S(2)}) copy-start(s32[2]{0:T(128)} %constant.64.clone) | copy-start | bytes 28
  128.7 261.4 %all-to-all-start.1 = ((bf16[16,33,64,256]{3,2,1,0:T(8,128)(2,1)}), bf16[16,33,64,256]{3,2,1,0:T(8,128)(2,1)}, u32[]{:S(2)}, u32[]{:S(2)}) async-start(bf16[16,33,64,256]{3,2,1,0:T(8,128)(2,1)} %bitcast.6), calls=%async_computation.1 | async-start | bytes 34603008 | tf_op jit(solution)/shard_map/all_to_all | solution.py:61
Sparse Core Ops, SparseCore 0:
  9.2 98.2 all-gather.1

commit v4 on v3

--- a/solution.py
+++ b/solution.py
@@ -58,7 +58,7 @@
     outgoing = jnp.take(column, picks.reshape(-1), axis=0, mode="clip").reshape(
         kv_count, pb_count * slots + 1, BLOCK, 2 * DH
     )
-    fetched = lax.all_to_all(outgoing, "kv", split_axis=0, concat_axis=0, tiled=True)
+    fetched = exchange(outgoing)
     tile_table = fetched.reshape(devices * slots + kv_count, BLOCK, 2 * DH)
     owner_of = selected // blocks_here
     positions = owner_of * slots + jnp.take(slot_rank.reshape(-1), selected)
@@ -73,6 +73,62 @@
 
 
 HEAD_GROUP = 4
+
+
+def exchange_kernel(out_hbm, fetched_hbm, send_sems, recv_sems, local_sem):
+    n = out_hbm.shape[0]
+    me = lax.axis_index("kv")
+    row = lax.axis_index("pb")
+    barrier = pltpu.get_barrier_semaphore()
+    for r in range(1, n):
+        pl.semaphore_signal(
+            barrier, inc=1, device_id=(row, lax.rem(me + r, n)), device_id_type=pl.DeviceIdType.MESH
+        )
+    pl.semaphore_wait(barrier, n - 1)
+    local = pltpu.make_async_copy(out_hbm.at[me], fetched_hbm.at[me], local_sem)
+    local.start()
+    sends = []
+    for r in range(1, n):
+        peer = lax.rem(me + r, n)
+        copy = pltpu.make_async_remote_copy(
+            src_ref=out_hbm.at[peer],
+            dst_ref=fetched_hbm.at[me],
+            send_sem=send_sems.at[r],
+            recv_sem=recv_sems.at[r],
+            device_id=(row, peer),
+            device_id_type=pl.DeviceIdType.MESH,
+        )
+        copy.start()
+        sends.append(copy)
+    for copy in sends:
+        copy.wait_send()
+    for r in range(1, n):
+        source = lax.rem(me + n - r, n)
+        pltpu.make_async_remote_copy(
+            src_ref=out_hbm.at[source],
+            dst_ref=fetched_hbm.at[source],
+            send_sem=send_sems.at[r],
+            recv_sem=recv_sems.at[r],
+            device_id=(row, source),
+            device_id_type=pl.DeviceIdType.MESH,
+        ).wait_recv()
+    local.wait()
+
+
+def exchange(outgoing):
+    n = outgoing.shape[0]
+    return pl.pallas_call(
+        exchange_kernel,
+        out_shape=jax.ShapeDtypeStruct(outgoing.shape, outgoing.dtype),
+        in_specs=[pl.BlockSpec(memory_space=pl.ANY)],
+        out_specs=pl.BlockSpec(memory_space=pl.ANY),
+        scratch_shapes=[
+            pltpu.SemaphoreType.DMA((n,)),
+            pltpu.SemaphoreType.DMA((n,)),
+            pltpu.SemaphoreType.DMA(()),
+        ],
+        compiler_params=pltpu.CompilerParams(collective_id=0, has_side_effects=True),
+    )(outgoing)
 
 
 def attend_kernel(pos_ref, q_ref, table_hbm, o_ref, kvbuf, sems):

time: 437 us -> 492 us (1.13)
  Pallas kernels: 34.5 us -> 353 us
  waiting for transfers between devices: 338 us -> 83 us
  starting transfers between devices: 14.6 us -> 7.34 us
    pallas_call x0 -> x1, Pallas kernels: none -> 318 us  [exchange(): pl.pallas_call(exchange_kernel, out_shape=jax.ShapeDtypeStruct(outgoing.s...]
    all_to_all x1 -> x0, waiting for transfers between devices: 250 us -> none  [per_device(): lax.all_to_all(outgoing, 'kv', split_axis=0, concat_axis=0, tiled=True)]
    all_to_all x1 -> x0, starting transfers between devices: 7.26 us -> none  [per_device(): lax.all_to_all(outgoing, 'kv', split_axis=0, concat_axis=0, tiled=True)]
  transfers between devices with their start and end apart: 3 -> 2, of which waited for: 3 -> 2; matrix products, arithmetic and copies ran while one was open for 2% -> 2% of each run, Pallas kernels for 0% -> 0%
where the time goes in v4:
time: 492 us; the launch traced here: 488 us
  Pallas kernels  353 us (72%)
  waiting for transfers between devices  83 us (17%)
  local copies, waits for them, and re-layouts  26.8 us (5%)
  between operations  13.5 us (3%)
  starting transfers between devices  7.34 us (1%)
    pallas_call x1, Pallas kernels, exchange(): pl.pallas_call(exchange_kernel, out_shape=jax.ShapeDtypeStruct(outgoing.s...  318 us
    all_gather x1, waiting for transfers between devices, per_device(): column = lax.all_gather(tiles_local, 'pb', axis=0, tiled=True)  83 us
    pallas_call x1, Pallas kernels, attend_blocks(): pl.pallas_call(attend_kernel, out_shape=jax.ShapeDtypeStruct(queries.shap...  34.5 us
    gather x1, local copies, waits for them, and re-layouts, per_device(): jnp.take(column, picks.reshape(-1), axis=0, mode='clip')  21.2 us
  transfers between devices with their start and end apart: 2, of which 2 were waited for; matrix products, arithmetic and copies ran while one was open for 2% of the time, Pallas kernels for 0%

profile of v4, /device:TPU:12, one launch (start us, length us, event | category | flops | bytes accessed | tf_op | source)
XLA Modules:
  0.0 488.2 jit_solution(14440881891856319152)
XLA Ops:
  6.5 2.3 pad_maximum_fusion
  8.9 0.1 add.62
  9.0 0.1 add.63
  9.0 0.8 copy.29
  9.8 0.1 eq.42
  9.9 1.7 convert_reduce_fusion
  11.8 0.1 copy.37
  11.9 0.1 reshape.112
  12.1 0.6 broadcast_add_fusion
  12.7 7.3 %all-to-all-start = ((s32[16,1,32]{2,1,0:T(1,128)}), s32[16,1,32]{2,1,0:T(1,128)S(1)}, u32[]{:S(2)}, u32[]{:S(2)}) async-start(s32[16,1,32]{2,1,0:T(1,128)} %bitcast.2), calls=%async_computation | async-start | bytes 16384 | tf_op jit(solution)/shard_map/all_to_all | solution.py:52
  20.0 0.1 copy.36
  20.1 0.7 pad.3.clone
  20.8 0.1 reshape.117
  20.9 0.1 sub.23
  21.0 2.5 gather_fusion
  23.5 0.1 reshape.116
  23.6 0.1 add_clamp_fusion
  23.7 0.6 min.12.pos_ref
  24.3 0.1 all-to-all-done
  24.4 0.1 reshape.125
  24.5 83.0 %all-gather.2.cloned.1.call-done = bf16[512,64,256]{2,1,0:T(8,128)(2,1)} async-done(((bf16[32,64,256]{2,1,0:T(8,128)(2,1)}), bf16[512,64,256]{2,1,0:T(8,128)(2,1)}) %all-gather.2.cloned.1.call-update) | async-done | bytes 16777232 | tf_op jit(solution)/shard_map/all_gather | solution.py:42
  107.5 21.2 %gather_fusion.1 = bf16[528,64,256]{2,1,0:T(8,128)(2,1)} fusion(bf16[512,64,256]{2,1,0:T(8,128)(2,1)} %all-gather.2.cloned.1.call-done, s32[1024]{0:T(1024)S(1)} %pad_clamp_fusion), kind=kCustom, calls=%fused_computation.1 | custom fusion | bytes 34605120 | tf_op jit(solution)/shard_map/jit(_take)/gather | solution.py:58
  128.7 318.1 %shard_map.55 = bf16[16,33,64,256]{3,2,1,0:T(8,128)(2,1)} custom-call(bf16[16,33,64,256]{3,2,1,0:T(8,128)(2,1)} %bitcast.6), custom_call_target="tpu_custom_call" | custom-call | tf_op jit(solution)/shard_map/pallas_call | solution.py:120
  446.8 34.5 %shard_map.56 = bf16[1536,1024]{1,0:T(8,128)(2,1)} custom-call(s32[384]{0:T(512)} %min.12.pos_ref, bf16[1536,1024]{1,0:T(8,128)(2,1)} %q_ref.1, bf16[528,64,256]{2,1,0:T(8,128)(2,1)} %bitcast.7), custom_call_target="tpu_custom_call" | custom-call | flops 6442450944 | bytes 18874368 | tf_op jit(solution)/shard_map/pallas_call | solution.py:177
  (14 shorter events, 0.2 us)
Async XLA Ops:
  6.5 100.9 %all-gather.2.cloned.1.call-start = ((), (), s32[]{:S(2)}) async-start(), calls=%async_computation.1 | async-start | bytes 17825792 | tf_op jit(solution)/shard_map/all_gather | solution.py:42
  12.7 11.7 %all-to-all-start = ((s32[16,1,32]{2,1,0:T(1,128)}), s32[16,1,32]{2,1,0:T(1,128)S(1)}, u32[]{:S(2)}, u32[]{:S(2)}) async-start(s32[16,1,32]{2,1,0:T(1,128)} %bitcast.2), calls=%async_computation | async-start | bytes 16384 | tf_op jit(solution)/shard_map/all_to_all | solution.py:52
Sparse Core Ops, SparseCore 0:
  9.2 98.2 all-gather.1

commit v5 on v3

--- a/solution.py
+++ b/solution.py
@@ -58,7 +58,7 @@
     outgoing = jnp.take(column, picks.reshape(-1), axis=0, mode="clip").reshape(
         kv_count, pb_count * slots + 1, BLOCK, 2 * DH
     )
-    fetched = lax.all_to_all(outgoing, "kv", split_axis=0, concat_axis=0, tiled=True)
+    fetched = exchange(outgoing)
     tile_table = fetched.reshape(devices * slots + kv_count, BLOCK, 2 * DH)
     owner_of = selected // blocks_here
     positions = owner_of * slots + jnp.take(slot_rank.reshape(-1), selected)
@@ -73,6 +73,116 @@
 
 
 HEAD_GROUP = 4
+
+
+SIDE = 4
+STEPS = [(dx, dy) for dy in range(SIDE) for dx in range(SIDE) if (dx, dy) != (0, 0)]
+DIRECT = [(dx, dy) for (dx, dy) in STEPS if dx != SIDE // 2 and dy != SIDE // 2]
+FAR = [(dx, dy) for (dx, dy) in STEPS if dx == SIDE // 2 or dy == SIDE // 2]
+
+
+def relays_of(dx, dy):
+    if dx == SIDE // 2 and dy == SIDE // 2:
+        return [(-1, -1), (1, 1)]
+    if dx == SIDE // 2:
+        return [(-1, 0), (1, 0)]
+    return [(0, -1), (0, 1)]
+
+
+def exchange_kernel(out_hbm, fetched_hbm, relay_hbm, d_send, d_recv, r_send, r_recv, f_send, f_recv, local_sem):
+    rows = out_hbm.shape[1]
+    parts = [(0, rows // 2), (rows // 2, rows - rows // 2)]
+    me = lax.axis_index("kv")
+    line = lax.axis_index("pb")
+    mx = me % SIDE
+    my = me // SIDE
+
+    def at(dx, dy):
+        return ((my + dy + SIDE) % SIDE) * SIDE + (mx + dx + SIDE) % SIDE
+
+    def remote(src, dst, send, recv, target):
+        return pltpu.make_async_remote_copy(
+            src_ref=src, dst_ref=dst, send_sem=send, recv_sem=recv,
+            device_id=(line, target), device_id_type=pl.DeviceIdType.MESH,
+        )
+
+    barrier = pltpu.get_barrier_semaphore()
+    for dx, dy in STEPS:
+        pl.semaphore_signal(
+            barrier, inc=1, device_id=(line, at(dx, dy)), device_id_type=pl.DeviceIdType.MESH
+        )
+    pl.semaphore_wait(barrier, len(STEPS))
+    local = pltpu.make_async_copy(out_hbm.at[me], fetched_hbm.at[me], local_sem)
+    local.start()
+    sent = []
+    for t, (dx, dy) in enumerate(FAR):
+        for h, (rx, ry) in enumerate(relays_of(dx, dy)):
+            f = 2 * t + h
+            lo, size = parts[h]
+            copy = remote(
+                out_hbm.at[at(dx, dy), pl.ds(lo, size)], relay_hbm.at[f, pl.ds(0, size)],
+                r_send.at[f], r_recv.at[f], at(rx, ry),
+            )
+            copy.start()
+            sent.append(copy)
+    for dx, dy in DIRECT:
+        k = dy * SIDE + dx
+        copy = remote(out_hbm.at[at(dx, dy)], fetched_hbm.at[me], d_send.at[k], d_recv.at[k], at(dx, dy))
+        copy.start()
+        sent.append(copy)
+    for t, (dx, dy) in enumerate(FAR):
+        for h, (rx, ry) in enumerate(relays_of(dx, dy)):
+            f = 2 * t + h
+            lo, size = parts[h]
+            held = relay_hbm.at[f, pl.ds(0, size)]
+            remote(held, held, r_send.at[f], r_recv.at[f], at(-rx, -ry)).wait_recv()
+            copy = remote(
+                held, fetched_hbm.at[at(-rx, -ry), pl.ds(lo, size)],
+                f_send.at[f], f_recv.at[f], at(dx - rx, dy - ry),
+            )
+            copy.start()
+            sent.append(copy)
+    for copy in sent:
+        copy.wait_send()
+    for dx, dy in DIRECT:
+        k = dy * SIDE + dx
+        source = at(-dx, -dy)
+        remote(
+            out_hbm.at[source], fetched_hbm.at[source], d_send.at[k], d_recv.at[k], source
+        ).wait_recv()
+    for t, (dx, dy) in enumerate(FAR):
+        for h in range(2):
+            f = 2 * t + h
+            lo, size = parts[h]
+            source = at(-dx, -dy)
+            part = fetched_hbm.at[source, pl.ds(lo, size)]
+            remote(part, part, f_send.at[f], f_recv.at[f], source).wait_recv()
+    local.wait()
+
+
+def exchange(outgoing):
+    n, rows = outgoing.shape[:2]
+    flows = 2 * len(FAR)
+    fetched, _ = pl.pallas_call(
+        exchange_kernel,
+        out_shape=(
+            jax.ShapeDtypeStruct(outgoing.shape, outgoing.dtype),
+            jax.ShapeDtypeStruct((flows, rows - rows // 2) + outgoing.shape[2:], outgoing.dtype),
+        ),
+        in_specs=[pl.BlockSpec(memory_space=pl.ANY)],
+        out_specs=(pl.BlockSpec(memory_space=pl.ANY), pl.BlockSpec(memory_space=pl.ANY)),
+        scratch_shapes=[
+            pltpu.SemaphoreType.DMA((n,)),
+            pltpu.SemaphoreType.DMA((n,)),
+            pltpu.SemaphoreType.DMA((flows,)),
+            pltpu.SemaphoreType.DMA((flows,)),
+            pltpu.SemaphoreType.DMA((flows,)),
+            pltpu.SemaphoreType.DMA((flows,)),
+            pltpu.SemaphoreType.DMA(()),
+        ],
+        compiler_params=pltpu.CompilerParams(collective_id=0, has_side_effects=True),
+    )(outgoing)
+    return fetched
 
 
 def attend_kernel(pos_ref, q_ref, table_hbm, o_ref, kvbuf, sems):

time: 437 us -> 434 us (level); the launches traced: 431 us -> 433 us
  Pallas kernels: 34.5 us -> 297 us
  waiting for transfers between devices: 338 us -> 83 us
  starting transfers between devices: 14.6 us -> 7.34 us
    pallas_call x0 -> x1, Pallas kernels: none -> 263 us  [exchange(): pl.pallas_call(exchange_kernel, out_shape=(jax.ShapeDtypeStruct(outgoing....]
    all_to_all x1 -> x0, waiting for transfers between devices: 250 us -> none  [per_device(): lax.all_to_all(outgoing, 'kv', split_axis=0, concat_axis=0, tiled=True)]
    all_to_all x1 -> x0, starting transfers between devices: 7.26 us -> none  [per_device(): lax.all_to_all(outgoing, 'kv', split_axis=0, concat_axis=0, tiled=True)]
    all_to_all x1, waiting for transfers between devices: 4.41 us -> 0.02 us  [per_device(): lax.all_to_all(by_column, 'kv', split_axis=0, concat_axis=0, tiled=True)]
  transfers between devices with their start and end apart: 3 -> 2, of which waited for: 3 -> 1; matrix products, arithmetic and copies ran while one was open for 2% -> 2% of each run, Pallas kernels for 0% -> 0%
where the time goes in v5:
time: 434 us; the launch traced here: 433 us
  Pallas kernels  297 us (68%)
  waiting for transfers between devices  83 us (19%)
  local copies, waits for them, and re-layouts  26.8 us (6%)
  between operations  13.5 us (3%)
  starting transfers between devices  7.34 us (2%)
  other arithmetic  4.89 us (1%)
    pallas_call x1, Pallas kernels, exchange(): pl.pallas_call(exchange_kernel, out_shape=(jax.ShapeDtypeStruct(outgoing....  263 us
    all_gather x1, waiting for transfers between devices, per_device(): column = lax.all_gather(tiles_local, 'pb', axis=0, tiled=True)  83 us
    pallas_call x1, Pallas kernels, attend_blocks(): pl.pallas_call(attend_kernel, out_shape=jax.ShapeDtypeStruct(queries.shap...  34.5 us
    gather x1, local copies, waits for them, and re-layouts, per_device(): jnp.take(column, picks.reshape(-1), axis=0, mode='clip')  21.2 us
  transfers between devices with their start and end apart: 2, of which 1 were waited for; matrix products, arithmetic and copies ran while one was open for 2% of the time, Pallas kernels for 0%

profile of v5, /device:TPU:12, one launch (start us, length us, event | category | flops | bytes accessed | tf_op | source)
XLA Modules:
  0.0 433.0 jit_solution(9535712349308356545)
XLA Ops:
  6.5 2.3 pad_maximum_fusion
  8.9 0.1 add.62
  9.0 0.1 add.63
  9.0 0.8 copy.29
  9.8 0.1 eq.42
  9.9 1.7 convert_reduce_fusion
  11.7 0.1 reduce_window_sum.11
  11.8 0.1 copy.37
  11.9 0.1 reshape.112
  12.1 0.6 broadcast_add_fusion
  12.7 7.3 %all-to-all-start = ((s32[16,1,32]{2,1,0:T(1,128)}), s32[16,1,32]{2,1,0:T(1,128)S(1)}, u32[]{:S(2)}, u32[]{:S(2)}) async-start(s32[16,1,32]{2,1,0:T(1,128)} %bitcast.2), calls=%async_computation | async-start | bytes 16384 | tf_op jit(solution)/shard_map/all_to_all | solution.py:52
  20.0 0.1 copy.36
  20.1 0.7 pad.3.clone
  20.8 0.1 reshape.117
  20.9 0.1 sub.23
  21.0 2.5 gather_fusion
  23.5 0.1 reshape.116
  23.6 0.1 add_clamp_fusion
  23.7 0.7 min.12.pos_ref
  24.4 0.1 reshape.125
  24.5 83.0 %all-gather.2.cloned.1.call-done = bf16[512,64,256]{2,1,0:T(8,128)(2,1)} async-done(((bf16[32,64,256]{2,1,0:T(8,128)(2,1)}), bf16[512,64,256]{2,1,0:T(8,128)(2,1)}) %all-gather.2.cloned.1.call-update) | async-done | bytes 16777232 | tf_op jit(solution)/shard_map/all_gather | solution.py:42
  107.5 21.2 %gather_fusion.1 = bf16[528,64,256]{2,1,0:T(8,128)(2,1)} fusion(bf16[512,64,256]{2,1,0:T(8,128)(2,1)} %all-gather.2.cloned.1.call-done, s32[1024]{0:T(1024)S(1)} %pad_clamp_fusion), kind=kCustom, calls=%fused_computation.1 | custom fusion | bytes 34605120 | tf_op jit(solution)/shard_map/jit(_take)/gather | solution.py:58
  128.7 262.9 %shard_map.55 = (bf16[16,33,64,256]{3,2,1,0:T(8,128)(2,1)}, bf16[14,17,64,256]{3,2,1,0:T(8,128)(2,1)}) custom-call(bf16[16,33,64,256]{3,2,1,0:T(8,128)(2,1)} %bitcast.6), custom_call_target="tpu_custom_call" | custom-call | tf_op jit(solution)/shard_map/pallas_call | solution.py:166
  391.6 34.5 %shard_map.56 = bf16[1536,1024]{1,0:T(8,128)(2,1)} custom-call(s32[384]{0:T(512)} %min.12.pos_ref, bf16[1536,1024]{1,0:T(8,128)(2,1)} %q_ref.1, bf16[528,64,256]{2,1,0:T(8,128)(2,1)} %bitcast.10), custom_call_target="tpu_custom_call" | custom-call | flops 6442450944 | bytes 18874368 | tf_op jit(solution)/shard_map/pallas_call | solution.py:231
  (14 shorter events, 0.1 us)
Async XLA Ops:
  6.5 100.9 %all-gather.2.cloned.1.call-start = ((), (), s32[]{:S(2)}) async-start(), calls=%async_computation.1 | async-start | bytes 17825792 | tf_op jit(solution)/shard_map/all_gather | solution.py:42
  12.7 11.7 %all-to-all-start = ((s32[16,1,32]{2,1,0:T(1,128)}), s32[16,1,32]{2,1,0:T(1,128)S(1)}, u32[]{:S(2)}, u32[]{:S(2)}) async-start(s32[16,1,32]{2,1,0:T(1,128)} %bitcast.2), calls=%async_computation | async-start | bytes 16384 | tf_op jit(solution)/shard_map/all_to_all | solution.py:52
Sparse Core Ops, SparseCore 0:
  9.2 98.2 all-gather.1

commit v6 on v5

--- a/solution.py
+++ b/solution.py
@@ -81,17 +81,17 @@
 FAR = [(dx, dy) for (dx, dy) in STEPS if dx == SIDE // 2 or dy == SIDE // 2]
 
 
-def relays_of(dx, dy):
-    if dx == SIDE // 2 and dy == SIDE // 2:
-        return [(-1, -1), (1, 1)]
-    if dx == SIDE // 2:
-        return [(-1, 0), (1, 0)]
-    return [(0, -1), (0, 1)]
+RELAY_DIR = -1
+RELAY_ROWS = 13
+
+
+def relay_of(dx, dy):
+    return (RELAY_DIR if dx == SIDE // 2 else 0, RELAY_DIR if dy == SIDE // 2 else 0)
 
 
 def exchange_kernel(out_hbm, fetched_hbm, relay_hbm, d_send, d_recv, r_send, r_recv, f_send, f_recv, local_sem):
     rows = out_hbm.shape[1]
-    parts = [(0, rows // 2), (rows // 2, rows - rows // 2)]
+    cut = RELAY_ROWS
     me = lax.axis_index("kv")
     line = lax.axis_index("pb")
     mx = me % SIDE
@@ -116,58 +116,55 @@
     local.start()
     sent = []
     for t, (dx, dy) in enumerate(FAR):
-        for h, (rx, ry) in enumerate(relays_of(dx, dy)):
-            f = 2 * t + h
-            lo, size = parts[h]
-            copy = remote(
-                out_hbm.at[at(dx, dy), pl.ds(lo, size)], relay_hbm.at[f, pl.ds(0, size)],
-                r_send.at[f], r_recv.at[f], at(rx, ry),
-            )
-            copy.start()
-            sent.append(copy)
-    for dx, dy in DIRECT:
+        rx, ry = relay_of(dx, dy)
+        copy = remote(
+            out_hbm.at[at(dx, dy), pl.ds(0, cut)], relay_hbm.at[t],
+            r_send.at[t], r_recv.at[t], at(rx, ry),
+        )
+        copy.start()
+        sent.append(copy)
+    for dx, dy in STEPS:
         k = dy * SIDE + dx
-        copy = remote(out_hbm.at[at(dx, dy)], fetched_hbm.at[me], d_send.at[k], d_recv.at[k], at(dx, dy))
+        lo = cut if (dx, dy) in FAR else 0
+        copy = remote(
+            out_hbm.at[at(dx, dy), pl.ds(lo, rows - lo)], fetched_hbm.at[me, pl.ds(lo, rows - lo)],
+            d_send.at[k], d_recv.at[k], at(dx, dy),
+        )
         copy.start()
         sent.append(copy)
     for t, (dx, dy) in enumerate(FAR):
-        for h, (rx, ry) in enumerate(relays_of(dx, dy)):
-            f = 2 * t + h
-            lo, size = parts[h]
-            held = relay_hbm.at[f, pl.ds(0, size)]
-            remote(held, held, r_send.at[f], r_recv.at[f], at(-rx, -ry)).wait_recv()
-            copy = remote(
-                held, fetched_hbm.at[at(-rx, -ry), pl.ds(lo, size)],
-                f_send.at[f], f_recv.at[f], at(dx - rx, dy - ry),
-            )
-            copy.start()
-            sent.append(copy)
+        rx, ry = relay_of(dx, dy)
+        held = relay_hbm.at[t]
+        remote(held, held, r_send.at[t], r_recv.at[t], at(-rx, -ry)).wait_recv()
+        copy = remote(
+            held, fetched_hbm.at[at(-rx, -ry), pl.ds(0, cut)],
+            f_send.at[t], f_recv.at[t], at(dx - rx, dy - ry),
+        )
+        copy.start()
+        sent.append(copy)
     for copy in sent:
         copy.wait_send()
-    for dx, dy in DIRECT:
+    for dx, dy in STEPS:
         k = dy * SIDE + dx
+        lo = cut if (dx, dy) in FAR else 0
         source = at(-dx, -dy)
-        remote(
-            out_hbm.at[source], fetched_hbm.at[source], d_send.at[k], d_recv.at[k], source
-        ).wait_recv()
+        part = fetched_hbm.at[source, pl.ds(lo, rows - lo)]
+        remote(part, part, d_send.at[k], d_recv.at[k], source).wait_recv()
     for t, (dx, dy) in enumerate(FAR):
-        for h in range(2):
-            f = 2 * t + h
-            lo, size = parts[h]
-            source = at(-dx, -dy)
-            part = fetched_hbm.at[source, pl.ds(lo, size)]
-            remote(part, part, f_send.at[f], f_recv.at[f], source).wait_recv()
+        source = at(-dx, -dy)
+        part = fetched_hbm.at[source, pl.ds(0, cut)]
+        remote(part, part, f_send.at[t], f_recv.at[t], source).wait_recv()
     local.wait()
 
 
 def exchange(outgoing):
     n, rows = outgoing.shape[:2]
-    flows = 2 * len(FAR)
+    flows = len(FAR)
     fetched, _ = pl.pallas_call(
         exchange_kernel,
         out_shape=(
             jax.ShapeDtypeStruct(outgoing.shape, outgoing.dtype),
-            jax.ShapeDtypeStruct((flows, rows - rows // 2) + outgoing.shape[2:], outgoing.dtype),
+            jax.ShapeDtypeStruct((flows, RELAY_ROWS) + outgoing.shape[2:], outgoing.dtype),
         ),
         in_specs=[pl.BlockSpec(memory_space=pl.ANY)],
         out_specs=(pl.BlockSpec(memory_space=pl.ANY), pl.BlockSpec(memory_space=pl.ANY)),

time: 434 us -> 466 us (1.074)
  Pallas kernels: 297 us -> 330 us
    pallas_call x1, Pallas kernels: 263 us -> 296 us  [exchange(): pl.pallas_call(exchange_kernel, out_shape=(jax.ShapeDtypeStruct(outgoing....]
where the time goes in v6:
time: 466 us
  Pallas kernels  330 us (71%)
  waiting for transfers between devices  83 us (18%)
  local copies, waits for them, and re-layouts  26.8 us (6%)
  between operations  13.5 us (3%)
  starting transfers between devices  7.34 us (2%)
  other arithmetic  4.89 us (1%)
    pallas_call x1, Pallas kernels, exchange(): pl.pallas_call(exchange_kernel, out_shape=(jax.ShapeDtypeStruct(outgoing....  296 us
    all_gather x1, waiting for transfers between devices, per_device(): column = lax.all_gather(tiles_local, 'pb', axis=0, tiled=True)  83 us
    pallas_call x1, Pallas kernels, attend_blocks(): pl.pallas_call(attend_kernel, out_shape=jax.ShapeDtypeStruct(queries.shap...  34.5 us
    gather x1, local copies, waits for them, and re-layouts, per_device(): jnp.take(column, picks.reshape(-1), axis=0, mode='clip')  21.2 us
  transfers between devices with their start and end apart: 2, of which 1 were waited for; matrix products, arithmetic and copies ran while one was open for 2% of the time, Pallas kernels for 0%

profile of v6, /device:TPU:12, one launch (start us, length us, event | category | flops | bytes accessed | tf_op | source)
XLA Modules:
  0.0 465.9 jit_solution(141586816195388547)
XLA Ops:
  6.5 2.3 pad_maximum_fusion
  8.9 0.1 add.62
  9.0 0.1 add.63
  9.0 0.8 copy.29
  9.8 0.1 eq.42
  9.9 1.7 convert_reduce_fusion
  11.7 0.1 reduce_window_sum.11
  11.8 0.1 copy.37
  11.9 0.1 reshape.112
  12.1 0.6 broadcast_add_fusion
  12.7 7.3 %all-to-all-start = ((s32[16,1,32]{2,1,0:T(1,128)}), s32[16,1,32]{2,1,0:T(1,128)S(1)}, u32[]{:S(2)}, u32[]{:S(2)}) async-start(s32[16,1,32]{2,1,0:T(1,128)} %bitcast.2), calls=%async_computation | async-start | bytes 16384 | tf_op jit(solution)/shard_map/all_to_all | solution.py:52
  20.0 0.1 copy.36
  20.1 0.7 pad.3.clone
  20.8 0.1 reshape.117
  20.9 0.1 sub.23
  21.0 2.5 gather_fusion
  23.5 0.1 reshape.116
  23.6 0.1 add_clamp_fusion
  23.7 0.7 min.12.pos_ref
  24.4 0.1 reshape.125
  24.5 83.0 %all-gather.2.cloned.1.call-done = bf16[512,64,256]{2,1,0:T(8,128)(2,1)} async-done(((bf16[32,64,256]{2,1,0:T(8,128)(2,1)}), bf16[512,64,256]{2,1,0:T(8,128)(2,1)}) %all-gather.2.cloned.1.call-update) | async-done | bytes 16777232 | tf_op jit(solution)/shard_map/all_gather | solution.py:42
  107.5 21.2 %gather_fusion.1 = bf16[528,64,256]{2,1,0:T(8,128)(2,1)} fusion(bf16[512,64,256]{2,1,0:T(8,128)(2,1)} %all-gather.2.cloned.1.call-done, s32[1024]{0:T(1024)S(1)} %pad_clamp_fusion), kind=kCustom, calls=%fused_computation.1 | custom fusion | bytes 34605120 | tf_op jit(solution)/shard_map/jit(_take)/gather | solution.py:58
  128.7 295.8 %shard_map.55 = (bf16[16,33,64,256]{3,2,1,0:T(8,128)(2,1)}, bf16[7,13,64,256]{3,2,1,0:T(8,128)(2,1)}) custom-call(bf16[16,33,64,256]{3,2,1,0:T(8,128)(2,1)} %bitcast.6), custom_call_target="tpu_custom_call" | custom-call | tf_op jit(solution)/shard_map/pallas_call | solution.py:163
  424.6 34.5 %shard_map.56 = bf16[1536,1024]{1,0:T(8,128)(2,1)} custom-call(s32[384]{0:T(512)} %min.12.pos_ref, bf16[1536,1024]{1,0:T(8,128)(2,1)} %q_ref.1, bf16[528,64,256]{2,1,0:T(8,128)(2,1)} %bitcast.10), custom_call_target="tpu_custom_call" | custom-call | flops 6442450944 | bytes 18874368 | tf_op jit(solution)/shard_map/pallas_call | solution.py:228
  (14 shorter events, 0.1 us)
Async XLA Ops:
  6.5 100.9 %all-gather.2.cloned.1.call-start = ((), (), s32[]{:S(2)}) async-start(), calls=%async_computation.1 | async-start | bytes 17825792 | tf_op jit(solution)/shard_map/all_gather | solution.py:42
  12.7 11.7 %all-to-all-start = ((s32[16,1,32]{2,1,0:T(1,128)}), s32[16,1,32]{2,1,0:T(1,128)S(1)}, u32[]{:S(2)}, u32[]{:S(2)}) async-start(s32[16,1,32]{2,1,0:T(1,128)} %bitcast.2), calls=%async_computation | async-start | bytes 16384 | tf_op jit(solution)/shard_map/all_to_all | solution.py:52
Sparse Core Ops, SparseCore 0:
  9.2 98.2 all-gather.1

commit v7 on v6

--- a/solution.py
+++ b/solution.py
@@ -81,7 +81,7 @@
 FAR = [(dx, dy) for (dx, dy) in STEPS if dx == SIDE // 2 or dy == SIDE // 2]
 
 
-RELAY_DIR = -1
+RELAY_DIR = 1
 RELAY_ROWS = 13
 
 

time: 466 us -> 449 us (0.964)
  Pallas kernels: 330 us -> 311 us
    pallas_call x1, Pallas kernels: 296 us -> 277 us  [exchange(): pl.pallas_call(exchange_kernel, out_shape=(jax.ShapeDtypeStruct(outgoing....]
where the time goes in v7:
time: 449 us; the launch traced here: 447 us
  Pallas kernels  311 us (69%)
  waiting for transfers between devices  83 us (18%)
  local copies, waits for them, and re-layouts  26.8 us (6%)
  between operations  13.5 us (3%)
  starting transfers between devices  7.34 us (2%)
  other arithmetic  4.89 us (1%)
    pallas_call x1, Pallas kernels, exchange(): pl.pallas_call(exchange_kernel, out_shape=(jax.ShapeDtypeStruct(outgoing....  277 us
    all_gather x1, waiting for transfers between devices, per_device(): column = lax.all_gather(tiles_local, 'pb', axis=0, tiled=True)  83 us
    pallas_call x1, Pallas kernels, attend_blocks(): pl.pallas_call(attend_kernel, out_shape=jax.ShapeDtypeStruct(queries.shap...  34.5 us
    gather x1, local copies, waits for them, and re-layouts, per_device(): jnp.take(column, picks.reshape(-1), axis=0, mode='clip')  21.2 us
  transfers between devices with their start and end apart: 2, of which 1 were waited for; matrix products, arithmetic and copies ran while one was open for 2% of the time, Pallas kernels for 0%

profile of v7, /device:TPU:12, one launch (start us, length us, event | category | flops | bytes accessed | tf_op | source)
XLA Modules:
  0.0 446.8 jit_solution(741709919578886653)
XLA Ops:
  6.5 2.3 pad_maximum_fusion
  8.9 0.1 add.62
  9.0 0.1 add.63
  9.0 0.8 copy.29
  9.8 0.1 eq.42
  9.9 1.7 convert_reduce_fusion
  11.7 0.1 reduce_window_sum.11
  11.8 0.1 copy.37
  11.9 0.1 reshape.112
  12.1 0.6 broadcast_add_fusion
  12.7 7.3 %all-to-all-start = ((s32[16,1,32]{2,1,0:T(1,128)}), s32[16,1,32]{2,1,0:T(1,128)S(1)}, u32[]{:S(2)}, u32[]{:S(2)}) async-start(s32[16,1,32]{2,1,0:T(1,128)} %bitcast.2), calls=%async_computation | async-start | bytes 16384 | tf_op jit(solution)/shard_map/all_to_all | solution.py:52
  20.0 0.1 copy.36
  20.1 0.7 pad.3.clone
  20.8 0.1 reshape.117
  20.9 0.1 sub.23
  21.0 2.5 gather_fusion
  23.5 0.1 reshape.116
  23.6 0.1 add_clamp_fusion
  23.7 0.7 min.12.pos_ref
  24.4 0.1 reshape.125
  24.5 83.0 %all-gather.2.cloned.1.call-done = bf16[512,64,256]{2,1,0:T(8,128)(2,1)} async-done(((bf16[32,64,256]{2,1,0:T(8,128)(2,1)}), bf16[512,64,256]{2,1,0:T(8,128)(2,1)}) %all-gather.2.cloned.1.call-update) | async-done | bytes 16777232 | tf_op jit(solution)/shard_map/all_gather | solution.py:42
  107.5 21.2 %gather_fusion.1 = bf16[528,64,256]{2,1,0:T(8,128)(2,1)} fusion(bf16[512,64,256]{2,1,0:T(8,128)(2,1)} %all-gather.2.cloned.1.call-done, s32[1024]{0:T(1024)S(1)} %pad_clamp_fusion), kind=kCustom, calls=%fused_computation.1 | custom fusion | bytes 34605120 | tf_op jit(solution)/shard_map/jit(_take)/gather | solution.py:58
  128.7 276.7 %shard_map.55 = (bf16[16,33,64,256]{3,2,1,0:T(8,128)(2,1)}, bf16[7,13,64,256]{3,2,1,0:T(8,128)(2,1)}) custom-call(bf16[16,33,64,256]{3,2,1,0:T(8,128)(2,1)} %bitcast.6), custom_call_target="tpu_custom_call" | custom-call | tf_op jit(solution)/shard_map/pallas_call | solution.py:163
  405.5 34.5 %shard_map.56 = bf16[1536,1024]{1,0:T(8,128)(2,1)} custom-call(s32[384]{0:T(512)} %min.12.pos_ref, bf16[1536,1024]{1,0:T(8,128)(2,1)} %q_ref.1, bf16[528,64,256]{2,1,0:T(8,128)(2,1)} %bitcast.10), custom_call_target="tpu_custom_call" | custom-call | flops 6442450944 | bytes 18874368 | tf_op jit(solution)/shard_map/pallas_call | solution.py:228
  (14 shorter events, 0.1 us)
Async XLA Ops:
  6.5 100.9 %all-gather.2.cloned.1.call-start = ((), (), s32[]{:S(2)}) async-start(), calls=%async_computation.1 | async-start | bytes 17825792 | tf_op jit(solution)/shard_map/all_gather | solution.py:42
  12.7 11.7 %all-to-all-start = ((s32[16,1,32]{2,1,0:T(1,128)}), s32[16,1,32]{2,1,0:T(1,128)S(1)}, u32[]{:S(2)}, u32[]{:S(2)}) async-start(s32[16,1,32]{2,1,0:T(1,128)} %bitcast.2), calls=%async_computation | async-start | bytes 16384 | tf_op jit(solution)/shard_map/all_to_all | solution.py:52
Sparse Core Ops, SparseCore 0:
  9.2 98.2 all-gather.1

commit v8 on v5

--- a/solution.py
+++ b/solution.py
@@ -72,7 +72,7 @@
     return attend_blocks(queries, tile_table, positions)
 
 
-HEAD_GROUP = 4
+HEAD_GROUP = 8
 
 
 SIDE = 4

time: 434 us -> 444 us (1.023)
  Pallas kernels: 297 us -> 307 us
    pallas_call x1, Pallas kernels: 34.5 us -> 44.1 us  [attend_blocks(): pl.pallas_call(attend_kernel, out_shape=jax.ShapeDtypeStruct(queries.shap...]
where the time goes in v8:
time: 444 us; the launch traced here: 443 us
  Pallas kernels  307 us (69%)
  waiting for transfers between devices  83 us (19%)
  local copies, waits for them, and re-layouts  26.8 us (6%)
  between operations  13.5 us (3%)
  starting transfers between devices  7.34 us (2%)
  other arithmetic  4.89 us (1%)
    pallas_call x1, Pallas kernels, exchange(): pl.pallas_call(exchange_kernel, out_shape=(jax.ShapeDtypeStruct(outgoing....  263 us
    all_gather x1, waiting for transfers between devices, per_device(): column = lax.all_gather(tiles_local, 'pb', axis=0, tiled=True)  83 us
    pallas_call x1, Pallas kernels, attend_blocks(): pl.pallas_call(attend_kernel, out_shape=jax.ShapeDtypeStruct(queries.shap...  44.1 us
    gather x1, local copies, waits for them, and re-layouts, per_device(): jnp.take(column, picks.reshape(-1), axis=0, mode='clip')  21.2 us
  transfers between devices with their start and end apart: 2, of which 1 were waited for; matrix products, arithmetic and copies ran while one was open for 2% of the time, Pallas kernels for 0%

profile of v8, /device:TPU:12, one launch (start us, length us, event | category | flops | bytes accessed | tf_op | source)
XLA Modules:
  0.0 442.5 jit_solution(10668991005669577009)
XLA Ops:
  6.5 2.3 pad_maximum_fusion
  8.9 0.1 add.62
  9.0 0.1 add.63
  9.0 0.8 copy.29
  9.8 0.1 eq.42
  9.9 1.7 convert_reduce_fusion
  11.7 0.1 reduce_window_sum.11
  11.8 0.1 copy.37
  11.9 0.1 reshape.112
  12.1 0.6 broadcast_add_fusion
  12.7 7.3 %all-to-all-start = ((s32[16,1,32]{2,1,0:T(1,128)}), s32[16,1,32]{2,1,0:T(1,128)S(1)}, u32[]{:S(2)}, u32[]{:S(2)}) async-start(s32[16,1,32]{2,1,0:T(1,128)} %bitcast.2), calls=%async_computation | async-start | bytes 16384 | tf_op jit(solution)/shard_map/all_to_all | solution.py:52
  20.0 0.1 copy.36
  20.1 0.7 pad.3.clone
  20.8 0.1 reshape.117
  20.9 0.1 sub.23
  21.0 2.5 gather_fusion
  23.5 0.1 reshape.116
  23.6 0.1 add_clamp_fusion
  23.7 0.7 min.12.pos_ref
  24.4 0.1 reshape.125
  24.5 83.0 %all-gather.2.cloned.1.call-done = bf16[512,64,256]{2,1,0:T(8,128)(2,1)} async-done(((bf16[32,64,256]{2,1,0:T(8,128)(2,1)}), bf16[512,64,256]{2,1,0:T(8,128)(2,1)}) %all-gather.2.cloned.1.call-update) | async-done | bytes 16777232 | tf_op jit(solution)/shard_map/all_gather | solution.py:42
  107.5 21.2 %gather_fusion.1 = bf16[528,64,256]{2,1,0:T(8,128)(2,1)} fusion(bf16[512,64,256]{2,1,0:T(8,128)(2,1)} %all-gather.2.cloned.1.call-done, s32[1024]{0:T(1024)S(1)} %pad_clamp_fusion), kind=kCustom, calls=%fused_computation.1 | custom fusion | bytes 34605120 | tf_op jit(solution)/shard_map/jit(_take)/gather | solution.py:58
  128.7 262.9 %shard_map.55 = (bf16[16,33,64,256]{3,2,1,0:T(8,128)(2,1)}, bf16[14,17,64,256]{3,2,1,0:T(8,128)(2,1)}) custom-call(bf16[16,33,64,256]{3,2,1,0:T(8,128)(2,1)} %bitcast.6), custom_call_target="tpu_custom_call" | custom-call | tf_op jit(solution)/shard_map/pallas_call | solution.py:166
  391.6 44.1 %shard_map.56 = bf16[1536,1024]{1,0:T(8,128)(2,1)} custom-call(s32[384]{0:T(512)} %min.12.pos_ref, bf16[1536,1024]{1,0:T(8,128)(2,1)} %q_ref.1, bf16[528,64,256]{2,1,0:T(8,128)(2,1)} %bitcast.10), custom_call_target="tpu_custom_call" | custom-call | flops 6442450944 | bytes 18874368 | tf_op jit(solution)/shard_map/pallas_call | solution.py:231
  (14 shorter events, 0.1 us)
Async XLA Ops:
  6.5 100.9 %all-gather.2.cloned.1.call-start = ((), (), s32[]{:S(2)}) async-start(), calls=%async_computation.1 | async-start | bytes 17825792 | tf_op jit(solution)/shard_map/all_gather | solution.py:42
  12.7 11.7 %all-to-all-start = ((s32[16,1,32]{2,1,0:T(1,128)}), s32[16,1,32]{2,1,0:T(1,128)S(1)}, u32[]{:S(2)}, u32[]{:S(2)}) async-start(s32[16,1,32]{2,1,0:T(1,128)} %bitcast.2), calls=%async_computation | async-start | bytes 16384 | tf_op jit(solution)/shard_map/all_to_all | solution.py:52
Sparse Core Ops, SparseCore 0:
  9.2 98.2 all-gather.1

commit v9 on v8

--- a/solution.py
+++ b/solution.py
@@ -72,7 +72,7 @@
     return attend_blocks(queries, tile_table, positions)
 
 
-HEAD_GROUP = 8
+HEAD_GROUP = 2
 
 
 SIDE = 4

time: 444 us -> 445 us (level)
  no operation moved by 1% of the time
where the time goes in v9:
time: 445 us; the launch traced here: 443 us
  Pallas kernels  308 us (69%)
  waiting for transfers between devices  83 us (19%)
  local copies, waits for them, and re-layouts  26.8 us (6%)
  between operations  13.5 us (3%)
  starting transfers between devices  7.34 us (2%)
  other arithmetic  4.89 us (1%)
    pallas_call x1, Pallas kernels, exchange(): pl.pallas_call(exchange_kernel, out_shape=(jax.ShapeDtypeStruct(outgoing....  263 us
    all_gather x1, waiting for transfers between devices, per_device(): column = lax.all_gather(tiles_local, 'pb', axis=0, tiled=True)  83 us
    pallas_call x1, Pallas kernels, attend_blocks(): pl.pallas_call(attend_kernel, out_shape=jax.ShapeDtypeStruct(queries.shap...  44.8 us
    gather x1, local copies, waits for them, and re-layouts, per_device(): jnp.take(column, picks.reshape(-1), axis=0, mode='clip')  21.2 us
  transfers between devices with their start and end apart: 2, of which 1 were waited for; matrix products, arithmetic and copies ran while one was open for 2% of the time, Pallas kernels for 0%

profile of v9, /device:TPU:12, one launch (start us, length us, event | category | flops | bytes accessed | tf_op | source)
XLA Modules:
  0.0 443.3 jit_solution(11227634515622250778)
XLA Ops:
  6.5 2.3 pad_maximum_fusion
  8.9 0.1 add.62
  9.0 0.1 add.63
  9.0 0.8 copy.29
  9.8 0.1 eq.42
  9.9 1.7 convert_reduce_fusion
  11.7 0.1 reduce_window_sum.11
  11.8 0.1 copy.37
  11.9 0.1 reshape.112
  12.1 0.6 broadcast_add_fusion
  12.7 7.3 %all-to-all-start = ((s32[16,1,32]{2,1,0:T(1,128)}), s32[16,1,32]{2,1,0:T(1,128)S(1)}, u32[]{:S(2)}, u32[]{:S(2)}) async-start(s32[16,1,32]{2,1,0:T(1,128)} %bitcast.2), calls=%async_computation | async-start | bytes 16384 | tf_op jit(solution)/shard_map/all_to_all | solution.py:52
  20.0 0.1 copy.36
  20.1 0.7 pad.3.clone
  20.8 0.1 reshape.117
  20.9 0.1 sub.23
  21.0 2.5 gather_fusion
  23.5 0.1 reshape.116
  23.6 0.1 add_clamp_fusion
  23.7 0.7 min.12.pos_ref
  24.4 0.1 reshape.125
  24.5 83.0 %all-gather.2.cloned.1.call-done = bf16[512,64,256]{2,1,0:T(8,128)(2,1)} async-done(((bf16[32,64,256]{2,1,0:T(8,128)(2,1)}), bf16[512,64,256]{2,1,0:T(8,128)(2,1)}) %all-gather.2.cloned.1.call-update) | async-done | bytes 16777232 | tf_op jit(solution)/shard_map/all_gather | solution.py:42
  107.5 21.2 %gather_fusion.1 = bf16[528,64,256]{2,1,0:T(8,128)(2,1)} fusion(bf16[512,64,256]{2,1,0:T(8,128)(2,1)} %all-gather.2.cloned.1.call-done, s32[1024]{0:T(1024)S(1)} %pad_clamp_fusion), kind=kCustom, calls=%fused_computation.1 | custom fusion | bytes 34605120 | tf_op jit(solution)/shard_map/jit(_take)/gather | solution.py:58
  128.7 262.9 %shard_map.55 = (bf16[16,33,64,256]{3,2,1,0:T(8,128)(2,1)}, bf16[14,17,64,256]{3,2,1,0:T(8,128)(2,1)}) custom-call(bf16[16,33,64,256]{3,2,1,0:T(8,128)(2,1)} %bitcast.6), custom_call_target="tpu_custom_call" | custom-call | tf_op jit(solution)/shard_map/pallas_call | solution.py:166
  391.6 44.8 %shard_map.56 = bf16[1536,1024]{1,0:T(8,128)(2,1)} custom-call(s32[384]{0:T(512)} %min.12.pos_ref, bf16[1536,1024]{1,0:T(8,128)(2,1)} %q_ref.1, bf16[528,64,256]{2,1,0:T(8,128)(2,1)} %bitcast.10), custom_call_target="tpu_custom_call" | custom-call | flops 6442450944 | bytes 18874368 | tf_op jit(solution)/shard_map/pallas_call | solution.py:231
  (14 shorter events, 0.1 us)
Async XLA Ops:
  6.5 100.9 %all-gather.2.cloned.1.call-start = ((), (), s32[]{:S(2)}) async-start(), calls=%async_computation.1 | async-start | bytes 17825792 | tf_op jit(solution)/shard_map/all_gather | solution.py:42
  12.7 11.7 %all-to-all-start = ((s32[16,1,32]{2,1,0:T(1,128)}), s32[16,1,32]{2,1,0:T(1,128)S(1)}, u32[]{:S(2)}, u32[]{:S(2)}) async-start(s32[16,1,32]{2,1,0:T(1,128)} %bitcast.2), calls=%async_computation | async-start | bytes 16384 | tf_op jit(solution)/shard_map/all_to_all | solution.py:52
Sparse Core Ops, SparseCore 0:
  9.2 98.2 all-gather.1

commit v10 on v5

--- a/solution.py
+++ b/solution.py
@@ -81,6 +81,9 @@
 FAR = [(dx, dy) for (dx, dy) in STEPS if dx == SIDE // 2 or dy == SIDE // 2]
 
 
+RELAY_ROWS = 8
+
+
 def relays_of(dx, dy):
     if dx == SIDE // 2 and dy == SIDE // 2:
         return [(-1, -1), (1, 1)]
@@ -91,7 +94,8 @@
 
 def exchange_kernel(out_hbm, fetched_hbm, relay_hbm, d_send, d_recv, r_send, r_recv, f_send, f_recv, local_sem):
     rows = out_hbm.shape[1]
-    parts = [(0, rows // 2), (rows // 2, rows - rows // 2)]
+    parts = [(0, RELAY_ROWS), (RELAY_ROWS, RELAY_ROWS)]
+    far_lo = 2 * RELAY_ROWS
     me = lax.axis_index("kv")
     line = lax.axis_index("pb")
     mx = me % SIDE
@@ -125,9 +129,13 @@
             )
             copy.start()
             sent.append(copy)
-    for dx, dy in DIRECT:
+    for dx, dy in STEPS:
         k = dy * SIDE + dx
-        copy = remote(out_hbm.at[at(dx, dy)], fetched_hbm.at[me], d_send.at[k], d_recv.at[k], at(dx, dy))
+        lo = far_lo if (dx, dy) in FAR else 0
+        copy = remote(
+            out_hbm.at[at(dx, dy), pl.ds(lo, rows - lo)], fetched_hbm.at[me, pl.ds(lo, rows - lo)],
+            d_send.at[k], d_recv.at[k], at(dx, dy),
+        )
         copy.start()
         sent.append(copy)
     for t, (dx, dy) in enumerate(FAR):
@@ -144,12 +152,12 @@
             sent.append(copy)
     for copy in sent:
         copy.wait_send()
-    for dx, dy in DIRECT:
+    for dx, dy in STEPS:
         k = dy * SIDE + dx
+        lo = far_lo if (dx, dy) in FAR else 0
         source = at(-dx, -dy)
-        remote(
-            out_hbm.at[source], fetched_hbm.at[source], d_send.at[k], d_recv.at[k], source
-        ).wait_recv()
+        part = fetched_hbm.at[source, pl.ds(lo, rows - lo)]
+        remote(part, part, d_send.at[k], d_recv.at[k], source).wait_recv()
     for t, (dx, dy) in enumerate(FAR):
         for h in range(2):
             f = 2 * t + h
@@ -167,7 +175,7 @@
         exchange_kernel,
         out_shape=(
             jax.ShapeDtypeStruct(outgoing.shape, outgoing.dtype),
-            jax.ShapeDtypeStruct((flows, rows - rows // 2) + outgoing.shape[2:], outgoing.dtype),
+            jax.ShapeDtypeStruct((flows, RELAY_ROWS) + outgoing.shape[2:], outgoing.dtype),
         ),
         in_specs=[pl.BlockSpec(memory_space=pl.ANY)],
         out_specs=(pl.BlockSpec(memory_space=pl.ANY), pl.BlockSpec(memory_space=pl.ANY)),

time: 434 us -> 439 us (1.012)
  no operation moved by 1% of the time
where the time goes in v10:
time: 439 us; the launch traced here: 434 us
  Pallas kernels  299 us (68%)
  waiting for transfers between devices  83 us (19%)
  local copies, waits for them, and re-layouts  26.8 us (6%)
  between operations  13.5 us (3%)
  starting transfers between devices  7.34 us (2%)
  other arithmetic  4.89 us (1%)
    pallas_call x1, Pallas kernels, exchange(): pl.pallas_call(exchange_kernel, out_shape=(jax.ShapeDtypeStruct(outgoing....  264 us
    all_gather x1, waiting for transfers between devices, per_device(): column = lax.all_gather(tiles_local, 'pb', axis=0, tiled=True)  83 us
    pallas_call x1, Pallas kernels, attend_blocks(): pl.pallas_call(attend_kernel, out_shape=jax.ShapeDtypeStruct(queries.shap...  34.5 us
    gather x1, local copies, waits for them, and re-layouts, per_device(): jnp.take(column, picks.reshape(-1), axis=0, mode='clip')  21.2 us
  transfers between devices with their start and end apart: 2, of which 1 were waited for; matrix products, arithmetic and copies ran while one was open for 2% of the time, Pallas kernels for 0%

profile of v10, /device:TPU:12, one launch (start us, length us, event | category | flops | bytes accessed | tf_op | source)
XLA Modules:
  0.0 434.5 jit_solution(5702555086309661136)
XLA Ops:
  6.5 2.3 pad_maximum_fusion
  8.9 0.1 add.62
  9.0 0.1 add.63
  9.0 0.8 copy.29
  9.8 0.1 eq.42
  9.9 1.7 convert_reduce_fusion
  11.7 0.1 reduce_window_sum.11
  11.8 0.1 copy.37
  11.9 0.1 reshape.112
  12.1 0.6 broadcast_add_fusion
  12.7 7.3 %all-to-all-start = ((s32[16,1,32]{2,1,0:T(1,128)}), s32[16,1,32]{2,1,0:T(1,128)S(1)}, u32[]{:S(2)}, u32[]{:S(2)}) async-start(s32[16,1,32]{2,1,0:T(1,128)} %bitcast.2), calls=%async_computation | async-start | bytes 16384 | tf_op jit(solution)/shard_map/all_to_all | solution.py:52
  20.0 0.1 copy.36
  20.1 0.7 pad.3.clone
  20.8 0.1 reshape.117
  20.9 0.1 sub.23
  21.0 2.5 gather_fusion
  23.5 0.1 reshape.116
  23.6 0.1 add_clamp_fusion
  23.7 0.7 min.12.pos_ref
  24.4 0.1 reshape.125
  24.5 83.0 %all-gather.2.cloned.1.call-done = bf16[512,64,256]{2,1,0:T(8,128)(2,1)} async-done(((bf16[32,64,256]{2,1,0:T(8,128)(2,1)}), bf16[512,64,256]{2,1,0:T(8,128)(2,1)}) %all-gather.2.cloned.1.call-update) | async-done | bytes 16777232 | tf_op jit(solution)/shard_map/all_gather | solution.py:42
  107.5 21.2 %gather_fusion.1 = bf16[528,64,256]{2,1,0:T(8,128)(2,1)} fusion(bf16[512,64,256]{2,1,0:T(8,128)(2,1)} %all-gather.2.cloned.1.call-done, s32[1024]{0:T(1024)S(1)} %pad_clamp_fusion), kind=kCustom, calls=%fused_computation.1 | custom fusion | bytes 34605120 | tf_op jit(solution)/shard_map/jit(_take)/gather | solution.py:58
  128.7 264.4 %shard_map.55 = (bf16[16,33,64,256]{3,2,1,0:T(8,128)(2,1)}, bf16[14,8,64,256]{3,2,1,0:T(8,128)(2,1)}) custom-call(bf16[16,33,64,256]{3,2,1,0:T(8,128)(2,1)} %bitcast.6), custom_call_target="tpu_custom_call" | custom-call | tf_op jit(solution)/shard_map/pallas_call | solution.py:174
  393.1 34.5 %shard_map.56 = bf16[1536,1024]{1,0:T(8,128)(2,1)} custom-call(s32[384]{0:T(512)} %min.12.pos_ref, bf16[1536,1024]{1,0:T(8,128)(2,1)} %q_ref.1, bf16[528,64,256]{2,1,0:T(8,128)(2,1)} %bitcast.10), custom_call_target="tpu_custom_call" | custom-call | flops 6442450944 | bytes 18874368 | tf_op jit(solution)/shard_map/pallas_call | solution.py:239
  (14 shorter events, 0.1 us)
Async XLA Ops:
  6.5 100.9 %all-gather.2.cloned.1.call-start = ((), (), s32[]{:S(2)}) async-start(), calls=%async_computation.1 | async-start | bytes 17825792 | tf_op jit(solution)/shard_map/all_gather | solution.py:42
  12.7 11.7 %all-to-all-start = ((s32[16,1,32]{2,1,0:T(1,128)}), s32[16,1,32]{2,1,0:T(1,128)S(1)}, u32[]{:S(2)}, u32[]{:S(2)}) async-start(s32[16,1,32]{2,1,0:T(1,128)} %bitcast.2), calls=%async_computation | async-start | bytes 16384 | tf_op jit(solution)/shard_map/all_to_all | solution.py:52
Sparse Core Ops, SparseCore 0:
  9.2 98.2 all-gather.1

commit v11 on v5

--- a/solution.py
+++ b/solution.py
@@ -114,34 +114,44 @@
     pl.semaphore_wait(barrier, len(STEPS))
     local = pltpu.make_async_copy(out_hbm.at[me], fetched_hbm.at[me], local_sem)
     local.start()
+    def chunk(lo, size, c):
+        first = size // 2
+        return (lo, first) if c == 0 else (lo + first, size - first)
+
     sent = []
-    for t, (dx, dy) in enumerate(FAR):
-        for h, (rx, ry) in enumerate(relays_of(dx, dy)):
-            f = 2 * t + h
-            lo, size = parts[h]
-            copy = remote(
-                out_hbm.at[at(dx, dy), pl.ds(lo, size)], relay_hbm.at[f, pl.ds(0, size)],
-                r_send.at[f], r_recv.at[f], at(rx, ry),
-            )
-            copy.start()
-            sent.append(copy)
+    for c in range(2):
+        for t, (dx, dy) in enumerate(FAR):
+            for h, (rx, ry) in enumerate(relays_of(dx, dy)):
+                f = 2 * t + h
+                g = 2 * f + c
+                lo, size = parts[h]
+                clo, csz = chunk(lo, size, c)
+                copy = remote(
+                    out_hbm.at[at(dx, dy), pl.ds(clo, csz)], relay_hbm.at[f, pl.ds(clo - lo, csz)],
+                    r_send.at[g], r_recv.at[g], at(rx, ry),
+                )
+                copy.start()
+                sent.append(copy)
     for dx, dy in DIRECT:
         k = dy * SIDE + dx
         copy = remote(out_hbm.at[at(dx, dy)], fetched_hbm.at[me], d_send.at[k], d_recv.at[k], at(dx, dy))
         copy.start()
         sent.append(copy)
-    for t, (dx, dy) in enumerate(FAR):
-        for h, (rx, ry) in enumerate(relays_of(dx, dy)):
-            f = 2 * t + h
-            lo, size = parts[h]
-            held = relay_hbm.at[f, pl.ds(0, size)]
-            remote(held, held, r_send.at[f], r_recv.at[f], at(-rx, -ry)).wait_recv()
-            copy = remote(
-                held, fetched_hbm.at[at(-rx, -ry), pl.ds(lo, size)],
-                f_send.at[f], f_recv.at[f], at(dx - rx, dy - ry),
-            )
-            copy.start()
-            sent.append(copy)
+    for c in range(2):
+        for t, (dx, dy) in enumerate(FAR):
+            for h, (rx, ry) in enumerate(relays_of(dx, dy)):
+                f = 2 * t + h
+                g = 2 * f + c
+                lo, size = parts[h]
+                clo, csz = chunk(lo, size, c)
+                held = relay_hbm.at[f, pl.ds(clo - lo, csz)]
+                remote(held, held, r_send.at[g], r_recv.at[g], at(-rx, -ry)).wait_recv()
+                copy = remote(
+                    held, fetched_hbm.at[at(-rx, -ry), pl.ds(clo, csz)],
+                    f_send.at[g], f_recv.at[g], at(dx - rx, dy - ry),
+                )
+                copy.start()
+                sent.append(copy)
     for copy in sent:
         copy.wait_send()
     for dx, dy in DIRECT:
@@ -155,14 +165,18 @@
             f = 2 * t + h
             lo, size = parts[h]
             source = at(-dx, -dy)
-            part = fetched_hbm.at[source, pl.ds(lo, size)]
-            remote(part, part, f_send.at[f], f_recv.at[f], source).wait_recv()
+            for c in range(2):
+                g = 2 * f + c
+                clo, csz = chunk(lo, size, c)
+                part = fetched_hbm.at[source, pl.ds(clo, csz)]
+                remote(part, part, f_send.at[g], f_recv.at[g], source).wait_recv()
     local.wait()
 
 
 def exchange(outgoing):
     n, rows = outgoing.shape[:2]
     flows = 2 * len(FAR)
+    pieces = 2 * flows
     fetched, _ = pl.pallas_call(
         exchange_kernel,
         out_shape=(
@@ -174,10 +188,10 @@
         scratch_shapes=[
             pltpu.SemaphoreType.DMA((n,)),
             pltpu.SemaphoreType.DMA((n,)),
-            pltpu.SemaphoreType.DMA((flows,)),
-            pltpu.SemaphoreType.DMA((flows,)),
-            pltpu.SemaphoreType.DMA((flows,)),
-            pltpu.SemaphoreType.DMA((flows,)),
+            pltpu.SemaphoreType.DMA((pieces,)),
+            pltpu.SemaphoreType.DMA((pieces,)),
+            pltpu.SemaphoreType.DMA((pieces,)),
+            pltpu.SemaphoreType.DMA((pieces,)),
             pltpu.SemaphoreType.DMA(()),
         ],
         compiler_params=pltpu.CompilerParams(collective_id=0, has_side_effects=True),

time: 434 us -> 427 us (0.984); the launches traced: 433 us -> 419 us
  Pallas kernels: 297 us -> 284 us
    pallas_call x1, Pallas kernels: 263 us -> 249 us  [exchange(): pl.pallas_call(exchange_kernel, out_shape=(jax.ShapeDtypeStruct(outgoing....]
where the time goes in v11:
time: 427 us; the launch traced here: 419 us
  Pallas kernels  284 us (67%)
  waiting for transfers between devices  83 us (19%)
  local copies, waits for them, and re-layouts  26.8 us (6%)
  between operations  13.5 us (3%)
  starting transfers between devices  7.34 us (2%)
  other arithmetic  4.89 us (1%)
    pallas_call x1, Pallas kernels, exchange(): pl.pallas_call(exchange_kernel, out_shape=(jax.ShapeDtypeStruct(outgoing....  249 us
    all_gather x1, waiting for transfers between devices, per_device(): column = lax.all_gather(tiles_local, 'pb', axis=0, tiled=True)  83 us
    pallas_call x1, Pallas kernels, attend_blocks(): pl.pallas_call(attend_kernel, out_shape=jax.ShapeDtypeStruct(queries.shap...  34.5 us
    gather x1, local copies, waits for them, and re-layouts, per_device(): jnp.take(column, picks.reshape(-1), axis=0, mode='clip')  21.2 us
  transfers between devices with their start and end apart: 2, of which 1 were waited for; matrix products, arithmetic and copies ran while one was open for 2% of the time, Pallas kernels for 0%

profile of v11, /device:TPU:12, one launch (start us, length us, event | category | flops | bytes accessed | tf_op | source)
XLA Modules:
  0.0 419.2 jit_solution(2452049251387932375)
XLA Ops:
  6.5 2.3 pad_maximum_fusion
  8.9 0.1 add.62
  9.0 0.1 add.63
  9.0 0.8 copy.29
  9.8 0.1 eq.42
  9.9 1.7 convert_reduce_fusion
  11.7 0.1 reduce_window_sum.11
  11.8 0.1 copy.37
  11.9 0.1 reshape.112
  12.1 0.6 broadcast_add_fusion
  12.7 7.3 %all-to-all-start = ((s32[16,1,32]{2,1,0:T(1,128)}), s32[16,1,32]{2,1,0:T(1,128)S(1)}, u32[]{:S(2)}, u32[]{:S(2)}) async-start(s32[16,1,32]{2,1,0:T(1,128)} %bitcast.2), calls=%async_computation | async-start | bytes 16384 | tf_op jit(solution)/shard_map/all_to_all | solution.py:52
  20.0 0.1 copy.36
  20.1 0.7 pad.3.clone
  20.8 0.1 reshape.117
  20.9 0.1 sub.23
  21.0 2.5 gather_fusion
  23.5 0.1 reshape.116
  23.6 0.1 add_clamp_fusion
  23.7 0.7 min.12.pos_ref
  24.4 0.1 reshape.125
  24.5 83.0 %all-gather.2.cloned.1.call-done = bf16[512,64,256]{2,1,0:T(8,128)(2,1)} async-done(((bf16[32,64,256]{2,1,0:T(8,128)(2,1)}), bf16[512,64,256]{2,1,0:T(8,128)(2,1)}) %all-gather.2.cloned.1.call-update) | async-done | bytes 16777232 | tf_op jit(solution)/shard_map/all_gather | solution.py:42
  107.5 21.2 %gather_fusion.1 = bf16[528,64,256]{2,1,0:T(8,128)(2,1)} fusion(bf16[512,64,256]{2,1,0:T(8,128)(2,1)} %all-gather.2.cloned.1.call-done, s32[1024]{0:T(1024)S(1)} %pad_clamp_fusion), kind=kCustom, calls=%fused_computation.1 | custom fusion | bytes 34605120 | tf_op jit(solution)/shard_map/jit(_take)/gather | solution.py:58
  128.7 249.1 %shard_map.55 = (bf16[16,33,64,256]{3,2,1,0:T(8,128)(2,1)}, bf16[14,17,64,256]{3,2,1,0:T(8,128)(2,1)}) custom-call(bf16[16,33,64,256]{3,2,1,0:T(8,128)(2,1)} %bitcast.6), custom_call_target="tpu_custom_call" | custom-call | tf_op jit(solution)/shard_map/pallas_call | solution.py:180
  377.8 34.5 %shard_map.56 = bf16[1536,1024]{1,0:T(8,128)(2,1)} custom-call(s32[384]{0:T(512)} %min.12.pos_ref, bf16[1536,1024]{1,0:T(8,128)(2,1)} %q_ref.1, bf16[528,64,256]{2,1,0:T(8,128)(2,1)} %bitcast.10), custom_call_target="tpu_custom_call" | custom-call | flops 6442450944 | bytes 18874368 | tf_op jit(solution)/shard_map/pallas_call | solution.py:245
  (14 shorter events, 0.1 us)
Async XLA Ops:
  6.5 100.9 %all-gather.2.cloned.1.call-start = ((), (), s32[]{:S(2)}) async-start(), calls=%async_computation.1 | async-start | bytes 17825792 | tf_op jit(solution)/shard_map/all_gather | solution.py:42
  12.7 11.7 %all-to-all-start = ((s32[16,1,32]{2,1,0:T(1,128)}), s32[16,1,32]{2,1,0:T(1,128)S(1)}, u32[]{:S(2)}, u32[]{:S(2)}) async-start(s32[16,1,32]{2,1,0:T(1,128)} %bitcast.2), calls=%async_computation | async-start | bytes 16384 | tf_op jit(solution)/shard_map/all_to_all | solution.py:52
Sparse Core Ops, SparseCore 0:
  9.2 98.2 all-gather.1

commit v12 on v11

--- a/solution.py
+++ b/solution.py
@@ -81,6 +81,9 @@
 FAR = [(dx, dy) for (dx, dy) in STEPS if dx == SIDE // 2 or dy == SIDE // 2]
 
 
+CHUNKS = 4
+
+
 def relays_of(dx, dy):
     if dx == SIDE // 2 and dy == SIDE // 2:
         return [(-1, -1), (1, 1)]
@@ -115,15 +118,15 @@
     local = pltpu.make_async_copy(out_hbm.at[me], fetched_hbm.at[me], local_sem)
     local.start()
     def chunk(lo, size, c):
-        first = size // 2
-        return (lo, first) if c == 0 else (lo + first, size - first)
+        step = size // CHUNKS
+        return (lo + c * step, step if c < CHUNKS - 1 else size - (CHUNKS - 1) * step)
 
     sent = []
-    for c in range(2):
+    for c in range(CHUNKS):
         for t, (dx, dy) in enumerate(FAR):
             for h, (rx, ry) in enumerate(relays_of(dx, dy)):
                 f = 2 * t + h
-                g = 2 * f + c
+                g = CHUNKS * f + c
                 lo, size = parts[h]
                 clo, csz = chunk(lo, size, c)
                 copy = remote(
@@ -137,11 +140,11 @@
         copy = remote(out_hbm.at[at(dx, dy)], fetched_hbm.at[me], d_send.at[k], d_recv.at[k], at(dx, dy))
         copy.start()
         sent.append(copy)
-    for c in range(2):
+    for c in range(CHUNKS):
         for t, (dx, dy) in enumerate(FAR):
             for h, (rx, ry) in enumerate(relays_of(dx, dy)):
                 f = 2 * t + h
-                g = 2 * f + c
+                g = CHUNKS * f + c
                 lo, size = parts[h]
                 clo, csz = chunk(lo, size, c)
                 held = relay_hbm.at[f, pl.ds(clo - lo, csz)]
@@ -165,8 +168,8 @@
             f = 2 * t + h
             lo, size = parts[h]
             source = at(-dx, -dy)
-            for c in range(2):
-                g = 2 * f + c
+            for c in range(CHUNKS):
+                g = CHUNKS * f + c
                 clo, csz = chunk(lo, size, c)
                 part = fetched_hbm.at[source, pl.ds(clo, csz)]
                 remote(part, part, f_send.at[g], f_recv.at[g], source).wait_recv()
@@ -176,7 +179,7 @@
 def exchange(outgoing):
     n, rows = outgoing.shape[:2]
     flows = 2 * len(FAR)
-    pieces = 2 * flows
+    pieces = CHUNKS * flows
     fetched, _ = pl.pallas_call(
         exchange_kernel,
         out_shape=(

time: 427 us -> 413 us (0.967)
  Pallas kernels: 284 us -> 273 us
    pallas_call x1, Pallas kernels: 249 us -> 238 us  [exchange(): pl.pallas_call(exchange_kernel, out_shape=(jax.ShapeDtypeStruct(outgoing....]
where the time goes in v12:
time: 413 us; the launch traced here: 408 us
  Pallas kernels  273 us (66%)
  waiting for transfers between devices  83 us (20%)
  local copies, waits for them, and re-layouts  26.8 us (6%)
  between operations  13.5 us (3%)
  starting transfers between devices  7.34 us (2%)
  other arithmetic  4.89 us (1%)
    pallas_call x1, Pallas kernels, exchange(): pl.pallas_call(exchange_kernel, out_shape=(jax.ShapeDtypeStruct(outgoing....  238 us
    all_gather x1, waiting for transfers between devices, per_device(): column = lax.all_gather(tiles_local, 'pb', axis=0, tiled=True)  83 us
    pallas_call x1, Pallas kernels, attend_blocks(): pl.pallas_call(attend_kernel, out_shape=jax.ShapeDtypeStruct(queries.shap...  34.5 us
    gather x1, local copies, waits for them, and re-layouts, per_device(): jnp.take(column, picks.reshape(-1), axis=0, mode='clip')  21.2 us
  transfers between devices with their start and end apart: 2, of which 1 were waited for; matrix products, arithmetic and copies ran while one was open for 2% of the time, Pallas kernels for 0%

profile of v12, /device:TPU:12, one launch (start us, length us, event | category | flops | bytes accessed | tf_op | source)
XLA Modules:
  0.0 408.1 jit_solution(635548061540706769)
XLA Ops:
  6.5 2.3 pad_maximum_fusion
  8.9 0.1 add.62
  9.0 0.1 add.63
  9.0 0.8 copy.29
  9.8 0.1 eq.42
  9.9 1.7 convert_reduce_fusion
  11.7 0.1 reduce_window_sum.11
  11.8 0.1 copy.37
  11.9 0.1 reshape.112
  12.1 0.6 broadcast_add_fusion
  12.7 7.3 %all-to-all-start = ((s32[16,1,32]{2,1,0:T(1,128)}), s32[16,1,32]{2,1,0:T(1,128)S(1)}, u32[]{:S(2)}, u32[]{:S(2)}) async-start(s32[16,1,32]{2,1,0:T(1,128)} %bitcast.2), calls=%async_computation | async-start | bytes 16384 | tf_op jit(solution)/shard_map/all_to_all | solution.py:52
  20.0 0.1 copy.36
  20.1 0.7 pad.3.clone
  20.8 0.1 reshape.117
  20.9 0.1 sub.23
  21.0 2.5 gather_fusion
  23.5 0.1 reshape.116
  23.6 0.1 add_clamp_fusion
  23.7 0.7 min.12.pos_ref
  24.4 0.1 reshape.125
  24.5 83.0 %all-gather.2.cloned.1.call-done = bf16[512,64,256]{2,1,0:T(8,128)(2,1)} async-done(((bf16[32,64,256]{2,1,0:T(8,128)(2,1)}), bf16[512,64,256]{2,1,0:T(8,128)(2,1)}) %all-gather.2.cloned.1.call-update) | async-done | bytes 16777232 | tf_op jit(solution)/shard_map/all_gather | solution.py:42
  107.5 21.2 %gather_fusion.1 = bf16[528,64,256]{2,1,0:T(8,128)(2,1)} fusion(bf16[512,64,256]{2,1,0:T(8,128)(2,1)} %all-gather.2.cloned.1.call-done, s32[1024]{0:T(1024)S(1)} %pad_clamp_fusion), kind=kCustom, calls=%fused_computation.1 | custom fusion | bytes 34605120 | tf_op jit(solution)/shard_map/jit(_take)/gather | solution.py:58
  128.7 238.0 %shard_map.55 = (bf16[16,33,64,256]{3,2,1,0:T(8,128)(2,1)}, bf16[14,17,64,256]{3,2,1,0:T(8,128)(2,1)}) custom-call(bf16[16,33,64,256]{3,2,1,0:T(8,128)(2,1)} %bitcast.6), custom_call_target="tpu_custom_call" | custom-call | tf_op jit(solution)/shard_map/pallas_call | solution.py:183
  366.7 34.5 %shard_map.56 = bf16[1536,1024]{1,0:T(8,128)(2,1)} custom-call(s32[384]{0:T(512)} %min.12.pos_ref, bf16[1536,1024]{1,0:T(8,128)(2,1)} %q_ref.1, bf16[528,64,256]{2,1,0:T(8,128)(2,1)} %bitcast.10), custom_call_target="tpu_custom_call" | custom-call | flops 6442450944 | bytes 18874368 | tf_op jit(solution)/shard_map/pallas_call | solution.py:248
  (14 shorter events, 0.1 us)
Async XLA Ops:
  6.5 100.9 %all-gather.2.cloned.1.call-start = ((), (), s32[]{:S(2)}) async-start(), calls=%async_computation.1 | async-start | bytes 17825792 | tf_op jit(solution)/shard_map/all_gather | solution.py:42
  12.7 11.7 %all-to-all-start = ((s32[16,1,32]{2,1,0:T(1,128)}), s32[16,1,32]{2,1,0:T(1,128)S(1)}, u32[]{:S(2)}, u32[]{:S(2)}) async-start(s32[16,1,32]{2,1,0:T(1,128)} %bitcast.2), calls=%async_computation | async-start | bytes 16384 | tf_op jit(solution)/shard_map/all_to_all | solution.py:52
Sparse Core Ops, SparseCore 0:
  9.2 98.2 all-gather.1

commit v13 on v12

--- a/solution.py
+++ b/solution.py
@@ -81,7 +81,7 @@
 FAR = [(dx, dy) for (dx, dy) in STEPS if dx == SIDE // 2 or dy == SIDE // 2]
 
 
-CHUNKS = 4
+CHUNKS = 8
 
 
 def relays_of(dx, dy):

time: 413 us -> 417 us (level)
  Pallas kernels: 273 us -> 279 us
    pallas_call x1, Pallas kernels: 238 us -> 244 us  [exchange(): pl.pallas_call(exchange_kernel, out_shape=(jax.ShapeDtypeStruct(outgoing....]
where the time goes in v13:
time: 417 us; the launch traced here: 414 us
  Pallas kernels  279 us (67%)
  waiting for transfers between devices  83 us (20%)
  local copies, waits for them, and re-layouts  26.8 us (6%)
  between operations  13.5 us (3%)
  starting transfers between devices  7.34 us (2%)
  other arithmetic  4.89 us (1%)
    pallas_call x1, Pallas kernels, exchange(): pl.pallas_call(exchange_kernel, out_shape=(jax.ShapeDtypeStruct(outgoing....  244 us
    all_gather x1, waiting for transfers between devices, per_device(): column = lax.all_gather(tiles_local, 'pb', axis=0, tiled=True)  83 us
    pallas_call x1, Pallas kernels, attend_blocks(): pl.pallas_call(attend_kernel, out_shape=jax.ShapeDtypeStruct(queries.shap...  34.5 us
    gather x1, local copies, waits for them, and re-layouts, per_device(): jnp.take(column, picks.reshape(-1), axis=0, mode='clip')  21.2 us
  transfers between devices with their start and end apart: 2, of which 1 were waited for; matrix products, arithmetic and copies ran while one was open for 2% of the time, Pallas kernels for 0%

profile of v13, /device:TPU:12, one launch (start us, length us, event | category | flops | bytes accessed | tf_op | source)
XLA Modules:
  0.0 414.2 jit_solution(10165917319778681928)
XLA Ops:
  6.5 2.3 pad_maximum_fusion
  8.9 0.1 add.62
  9.0 0.1 add.63
  9.0 0.8 copy.29
  9.8 0.1 eq.42
  9.9 1.7 convert_reduce_fusion
  11.7 0.1 reduce_window_sum.11
  11.8 0.1 copy.37
  11.9 0.1 reshape.112
  12.1 0.6 broadcast_add_fusion
  12.7 7.3 %all-to-all-start = ((s32[16,1,32]{2,1,0:T(1,128)}), s32[16,1,32]{2,1,0:T(1,128)S(1)}, u32[]{:S(2)}, u32[]{:S(2)}) async-start(s32[16,1,32]{2,1,0:T(1,128)} %bitcast.2), calls=%async_computation | async-start | bytes 16384 | tf_op jit(solution)/shard_map/all_to_all | solution.py:52
  20.0 0.1 copy.36
  20.1 0.7 pad.3.clone
  20.8 0.1 reshape.117
  20.9 0.1 sub.23
  21.0 2.5 gather_fusion
  23.5 0.1 reshape.116
  23.6 0.1 add_clamp_fusion
  23.7 0.7 min.12.pos_ref
  24.4 0.1 reshape.125
  24.5 83.0 %all-gather.2.cloned.1.call-done = bf16[512,64,256]{2,1,0:T(8,128)(2,1)} async-done(((bf16[32,64,256]{2,1,0:T(8,128)(2,1)}), bf16[512,64,256]{2,1,0:T(8,128)(2,1)}) %all-gather.2.cloned.1.call-update) | async-done | bytes 16777232 | tf_op jit(solution)/shard_map/all_gather | solution.py:42
  107.5 21.2 %gather_fusion.1 = bf16[528,64,256]{2,1,0:T(8,128)(2,1)} fusion(bf16[512,64,256]{2,1,0:T(8,128)(2,1)} %all-gather.2.cloned.1.call-done, s32[1024]{0:T(1024)S(1)} %pad_clamp_fusion), kind=kCustom, calls=%fused_computation.1 | custom fusion | bytes 34605120 | tf_op jit(solution)/shard_map/jit(_take)/gather | solution.py:58
  128.7 244.1 %shard_map.55 = (bf16[16,33,64,256]{3,2,1,0:T(8,128)(2,1)}, bf16[14,17,64,256]{3,2,1,0:T(8,128)(2,1)}) custom-call(bf16[16,33,64,256]{3,2,1,0:T(8,128)(2,1)} %bitcast.6), custom_call_target="tpu_custom_call" | custom-call | tf_op jit(solution)/shard_map/pallas_call | solution.py:183
  372.8 34.5 %shard_map.56 = bf16[1536,1024]{1,0:T(8,128)(2,1)} custom-call(s32[384]{0:T(512)} %min.12.pos_ref, bf16[1536,1024]{1,0:T(8,128)(2,1)} %q_ref.1, bf16[528,64,256]{2,1,0:T(8,128)(2,1)} %bitcast.10), custom_call_target="tpu_custom_call" | custom-call | flops 6442450944 | bytes 18874368 | tf_op jit(solution)/shard_map/pallas_call | solution.py:248
  (14 shorter events, 0.1 us)
Async XLA Ops:
  6.5 100.9 %all-gather.2.cloned.1.call-start = ((), (), s32[]{:S(2)}) async-start(), calls=%async_computation.1 | async-start | bytes 17825792 | tf_op jit(solution)/shard_map/all_gather | solution.py:42
  12.7 11.7 %all-to-all-start = ((s32[16,1,32]{2,1,0:T(1,128)}), s32[16,1,32]{2,1,0:T(1,128)S(1)}, u32[]{:S(2)}, u32[]{:S(2)}) async-start(s32[16,1,32]{2,1,0:T(1,128)} %bitcast.2), calls=%async_computation | async-start | bytes 16384 | tf_op jit(solution)/shard_map/all_to_all | solution.py:52
Sparse Core Ops, SparseCore 0:
  9.2 98.2 all-gather.1

commit v14 on v13

--- a/solution.py
+++ b/solution.py
@@ -81,7 +81,7 @@
 FAR = [(dx, dy) for (dx, dy) in STEPS if dx == SIDE // 2 or dy == SIDE // 2]
 
 
-CHUNKS = 8
+CHUNKS = 6
 
 
 def relays_of(dx, dy):

time: 417 us -> 417 us (level)
  no operation moved by 1% of the time
where the time goes in v14:
time: 417 us; the launch traced here: 415 us
  Pallas kernels  279 us (67%)
  waiting for transfers between devices  83 us (20%)
  local copies, waits for them, and re-layouts  26.8 us (6%)
  between operations  13.5 us (3%)
  starting transfers between devices  7.34 us (2%)
  other arithmetic  4.89 us (1%)
    pallas_call x1, Pallas kernels, exchange(): pl.pallas_call(exchange_kernel, out_shape=(jax.ShapeDtypeStruct(outgoing....  245 us
    all_gather x1, waiting for transfers between devices, per_device(): column = lax.all_gather(tiles_local, 'pb', axis=0, tiled=True)  83 us
    pallas_call x1, Pallas kernels, attend_blocks(): pl.pallas_call(attend_kernel, out_shape=jax.ShapeDtypeStruct(queries.shap...  34.5 us
    gather x1, local copies, waits for them, and re-layouts, per_device(): jnp.take(column, picks.reshape(-1), axis=0, mode='clip')  21.2 us
  transfers between devices with their start and end apart: 2, of which 1 were waited for; matrix products, arithmetic and copies ran while one was open for 2% of the time, Pallas kernels for 0%

profile of v14, /device:TPU:12, one launch (start us, length us, event | category | flops | bytes accessed | tf_op | source)
XLA Modules:
  0.0 414.9 jit_solution(1212330524024916973)
XLA Ops:
  6.5 2.3 pad_maximum_fusion
  8.9 0.1 add.62
  9.0 0.1 add.63
  9.0 0.8 copy.29
  9.8 0.1 eq.42
  9.9 1.7 convert_reduce_fusion
  11.7 0.1 reduce_window_sum.11
  11.8 0.1 copy.37
  11.9 0.1 reshape.112
  12.1 0.6 broadcast_add_fusion
  12.7 7.3 %all-to-all-start = ((s32[16,1,32]{2,1,0:T(1,128)}), s32[16,1,32]{2,1,0:T(1,128)S(1)}, u32[]{:S(2)}, u32[]{:S(2)}) async-start(s32[16,1,32]{2,1,0:T(1,128)} %bitcast.2), calls=%async_computation | async-start | bytes 16384 | tf_op jit(solution)/shard_map/all_to_all | solution.py:52
  20.0 0.1 copy.36
  20.1 0.7 pad.3.clone
  20.8 0.1 reshape.117
  20.9 0.1 sub.23
  21.0 2.5 gather_fusion
  23.5 0.1 reshape.116
  23.6 0.1 add_clamp_fusion
  23.7 0.7 min.12.pos_ref
  24.4 0.1 reshape.125
  24.5 83.0 %all-gather.2.cloned.1.call-done = bf16[512,64,256]{2,1,0:T(8,128)(2,1)} async-done(((bf16[32,64,256]{2,1,0:T(8,128)(2,1)}), bf16[512,64,256]{2,1,0:T(8,128)(2,1)}) %all-gather.2.cloned.1.call-update) | async-done | bytes 16777232 | tf_op jit(solution)/shard_map/all_gather | solution.py:42
  107.5 21.2 %gather_fusion.1 = bf16[528,64,256]{2,1,0:T(8,128)(2,1)} fusion(bf16[512,64,256]{2,1,0:T(8,128)(2,1)} %all-gather.2.cloned.1.call-done, s32[1024]{0:T(1024)S(1)} %pad_clamp_fusion), kind=kCustom, calls=%fused_computation.1 | custom fusion | bytes 34605120 | tf_op jit(solution)/shard_map/jit(_take)/gather | solution.py:58
  128.7 244.8 %shard_map.55 = (bf16[16,33,64,256]{3,2,1,0:T(8,128)(2,1)}, bf16[14,17,64,256]{3,2,1,0:T(8,128)(2,1)}) custom-call(bf16[16,33,64,256]{3,2,1,0:T(8,128)(2,1)} %bitcast.6), custom_call_target="tpu_custom_call" | custom-call | tf_op jit(solution)/shard_map/pallas_call | solution.py:183
  373.5 34.5 %shard_map.56 = bf16[1536,1024]{1,0:T(8,128)(2,1)} custom-call(s32[384]{0:T(512)} %min.12.pos_ref, bf16[1536,1024]{1,0:T(8,128)(2,1)} %q_ref.1, bf16[528,64,256]{2,1,0:T(8,128)(2,1)} %bitcast.10), custom_call_target="tpu_custom_call" | custom-call | flops 6442450944 | bytes 18874368 | tf_op jit(solution)/shard_map/pallas_call | solution.py:248
  (14 shorter events, 0.1 us)
Async XLA Ops:
  6.5 100.9 %all-gather.2.cloned.1.call-start = ((), (), s32[]{:S(2)}) async-start(), calls=%async_computation.1 | async-start | bytes 17825792 | tf_op jit(solution)/shard_map/all_gather | solution.py:42
  12.7 11.7 %all-to-all-start = ((s32[16,1,32]{2,1,0:T(1,128)}), s32[16,1,32]{2,1,0:T(1,128)S(1)}, u32[]{:S(2)}, u32[]{:S(2)}) async-start(s32[16,1,32]{2,1,0:T(1,128)} %bitcast.2), calls=%async_computation | async-start | bytes 16384 | tf_op jit(solution)/shard_map/all_to_all | solution.py:52
Sparse Core Ops, SparseCore 0:
  9.2 98.2 all-gather.1
